TPU v7x, 32 devices: a whole 2x2x4 slice. The times are simulated.
32 devices in a mesh: groups: 2 (over y), cells: 4 (over z), nodes: 2 (over x), sub: 2 (over core).
Axes of the slice: x: 2, y: 2, z: 4, core: 2. Of those that a mesh axis runs over, the one named last changes fastest.
Arguments:
- adjoint_start: float32 [4, 5, 16384], P('nodes', None, ('groups', 'cells', 'sub')), parts along dimension 2, may hold values from -6 to 6
- adjoint_rhs: float32 [4, 5, 16384], P('nodes', None, ('groups', 'cells', 'sub')), parts along dimension 2, may hold values from -6 to 6
- off_blocks: bfloat16 [4, 6, 25, 16384], P('nodes', None, None, ('groups', 'cells', 'sub')), parts along dimension 3, may hold values from -0.5 to 0.5
- diag_inverse: float32 [4, 25, 16384], P('nodes', None, ('groups', 'cells', 'sub')), parts along dimension 2, may hold values from -2.4 to 2.4
- neighbours: int32 [6, 8192], P(None, ('cells', 'sub')), may hold values from -1 to 8191, as said below
- node_weights: float32 [4], P('nodes'), may hold values from 0.05 to 0.5
- sens_blocks: bfloat16 [4, 15, 16384], P('nodes', None, ('groups', 'cells', 'sub')), parts along dimension 2, may hold values from -1.796875 to 1.796875
- cell_points: float32 [3, 8192], P(None, ('cells', 'sub')), may hold values from 0 to 1
- base_points: float32 [3, 4096], replicated, may hold values from 0 to 1
- ffd_index: int32 [4096, 8], replicated, may hold values from 0 to 511
- ffd_weight: float32 [4096, 8], replicated, may hold values from 0 to 1
Outputs:
- adjoint: float32 [4, 5, 16384], P('nodes', None, ('groups', 'cells', 'sub')), parts along dimension 2
- control_grad: float32 [6, 512], P('groups'), parts along dimension 0
There are 2 independent parts, one for each index of `groups`. A program takes and returns all parts, laid end to end along the dimension named above; an argument that names none is the same for every part. Nothing has to cross between parts.
Inputs may be any that keep to these rules, and one draw needn't show every extreme that they name: `neighbours`: each entry is -1 (no neighbour) or the index of a cell at most 1024 away from the cell; the distance 1024 occurs.
All inputs are finite; a program needn't handle non-finite values.
Results may differ from a plain program's by a relative error of at most 0.0003.
Values sent between devices are 32-bit elements; how exact they have to be, the bound alone decides.
A program may use at most 64 MiB of HBM per device.

v0:
```python
import functools

import jax
import jax.numpy as jnp
from jax import lax
from jax.experimental import pallas as pl
from jax.experimental.pallas import tpu as pltpu
from jax.sharding import PartitionSpec as P

SWEEPS = 2
FFD = 512
LANES = 128
ROWS = 8
TILE = 256

support_radius = 0.3
MESH = pl.DeviceIdType.MESH


def split2(x):
    hi = x.astype(jnp.bfloat16)
    return hi, (x - hi.astype(jnp.float32)).astype(jnp.bfloat16)


def split3(x):
    one = x.astype(jnp.bfloat16).astype(jnp.float32)
    two = (x - one).astype(jnp.bfloat16).astype(jnp.float32)
    return one, two, (x - one) - two


def kernel(
    scale,
    weight_ref,
    adj_hbm,
    point_hbm,
    nb_hbm,
    base_hbm,
    off_hbm,
    rhs_hbm,
    inv_hbm,
    sens_hbm,
    ffd_index_hbm,
    ffd_weight_hbm,
    out_ref,
    grad_ref,
    point_ref,
    nb_ref,
    base_ref,
    off_ref,
    rhs_ref,
    inv_ref,
    sens_ref,
    ffd_index_ref,
    ffd_weight_ref,
    wide,
    win,
    rel_ref,
    lane_ref,
    points,
    cell_feat,
    base_feat,
    k_hi,
    k_lo,
    l_hi,
    l_lo,
    sens_rows,
    sens_slots,
    sens_mat,
    grad_slots,
    load_sem,
    halo_send,
    halo_recv,
    point_send,
    point_recv,
    sens_send,
    sens_recv,
    grad_send,
    grad_recv,
    known,
):
    cells, subs, nodes = (lax.axis_size(a) for a in ("cells", "sub", "nodes"))
    cell_at, sub_at, node_at = (lax.axis_index(a) for a in ("cells", "sub", "nodes"))
    here, places = cell_at * subs + sub_at, cells * subs
    team, crew = node_at * subs + sub_at, nodes * subs
    me, everyone = cell_at * crew + team, cells * crew
    nodes_here = weight_ref.shape[0]
    rows = adj_hbm.shape[1]
    blocks = rows // nodes_here
    cell_count = blocks * LANES
    base_own = base_feat.shape[1]

    def member(index):
        return {"nodes": index // subs, "sub": index % subs}

    def anyone(index):
        return dict(member(index % crew), cells=index // crew)

    lower, upper = cell_at > 0, cell_at < cells - 1
    below, above = cell_at - 1, cell_at + 1

    barrier = pltpu.get_barrier_semaphore()

    def greet(device):
        pl.semaphore_signal(barrier, inc=1, device_id=device, device_id_type=MESH)

    greeted = crew - 1
    for step in range(1, crew):
        greet(member((team + step) % crew))
    greetings = [(lower, {"cells": below}), (upper, {"cells": above})]
    if subs > 1:
        first, last = sub_at == 0, sub_at == subs - 1
        greetings.append((jnp.logical_and(lower, first), {"cells": below, "sub": subs - 1}))
        greetings.append((jnp.logical_and(upper, last), {"cells": above, "sub": 0}))
    for exists, device in greetings:
        pl.when(exists)(functools.partial(greet, device))
        greeted = greeted + exists.astype(jnp.int32)

    base_start = pl.multiple_of(team * base_own, LANES)
    share = pl.ds(base_start, base_own)
    sources = (
        (adj_hbm, wide.at[0, :, pl.ds(rows, rows), :]),
        (point_hbm, point_ref),
        (nb_hbm, nb_ref),
        (base_hbm.at[:, share], base_ref),
        (off_hbm, off_ref),
        (rhs_hbm, rhs_ref),
        (inv_hbm, inv_ref),
        (sens_hbm, sens_ref),
        (ffd_index_hbm.at[:, share], ffd_index_ref),
        (ffd_weight_hbm.at[:, share], ffd_weight_ref),
    )
    loads = [
        pltpu.make_async_copy(source, target, load_sem.at[slot])
        for slot, (source, target) in enumerate(sources)
    ]
    for load in loads:
        load.start()
    (adj_load, point_load, nb_load, base_load, off_load, rhs_load, inv_load, sens_load) = loads[:8]

    def tell(stage):
        for side, (exists, other) in enumerate(((upper, above), (lower, below))):

            @pl.when(exists)
            def _():
                pl.semaphore_signal(
                    known.at[stage, side],
                    inc=1,
                    device_id={"cells": other},
                    device_id_type=MESH,
                )

    def hear(stage):
        for side, exists in enumerate((lower, upper)):

            @pl.when(exists)
            def _():
                pl.semaphore_wait(known.at[stage, side], 1)

    nb_load.wait()
    first_cell = here * cell_count
    for face in range(nb_ref.shape[0]):
        for block in range(blocks):
            entry = nb_ref[face : face + 1, block * LANES : (block + 1) * LANES]
            local = entry - first_cell + cell_count
            chunk = jnp.where(entry >= 0, (local >> 7) - block, -1)
            span = pl.ds(block * nodes_here, nodes_here)
            rel_ref[face, span, :] = jnp.broadcast_to(chunk, (nodes_here, LANES))
            lane_ref[face, span, :] = jnp.broadcast_to(local & (LANES - 1), (nodes_here, LANES))

    def build_lattice(step, carry):
        target = pl.ds(pl.multiple_of(step * LANES, LANES), LANES)
        index = ffd_index_ref[:, target]
        weight = ffd_weight_ref[:, target]
        group = 64
        row = lax.broadcasted_iota(jnp.int32, (group, LANES), 0)
        for top in range(0, FFD, group):
            total = jnp.zeros((group, LANES), jnp.float32)
            for slot in range(index.shape[0]):
                match = row == index[slot : slot + 1, :] - top
                total = total + jnp.where(match, weight[slot : slot + 1, :], 0.0)
            hi, lo = split2(total)
            l_hi[top : top + group, target] = hi
            l_lo[top : top + group, target] = lo
        return carry


    @pl.when(here == 0)
    def _():
        wide[:, :, 0:rows, :] = jnp.zeros((SWEEPS, 5, rows, LANES), jnp.float32)

    @pl.when(here == places - 1)
    def _():
        wide[:, :, 2 * rows : 3 * rows, :] = jnp.zeros((SWEEPS, 5, rows, LANES), jnp.float32)

    adj_load.wait()
    point_load.wait()
    pl.semaphore_wait(barrier, greeted)

    def halo(sweep, side):
        other = here + 1 if side == 0 else here - 1
        start = 0 if side == 0 else 2 * rows
        return pltpu.make_async_remote_copy(
            src_ref=wide.at[sweep, :, pl.ds(rows, rows), :],
            dst_ref=wide.at[sweep, :, pl.ds(start, rows), :],
            send_sem=halo_send.at[sweep, side],
            recv_sem=halo_recv.at[sweep, side],
            device_id={"cells": other // subs, "sub": other % subs},
            device_id_type=MESH,
        )

    def halo_start(sweep):
        @pl.when(here < places - 1)
        def _():
            halo(sweep, 0).start()

        @pl.when(here > 0)
        def _():
            halo(sweep, 1).start()

    def halo_wait(sweep):
        @pl.when(here > 0)
        def _():
            halo(sweep, 0).wait_recv()

        @pl.when(here < places - 1)
        def _():
            halo(sweep, 1).wait_recv()

    def halo_sent(sweep):
        @pl.when(here < places - 1)
        def _():
            halo(sweep, 0).wait_send()

        @pl.when(here > 0)
        def _():
            halo(sweep, 1).wait_send()

    def point_copy(step):
        return pltpu.make_async_remote_copy(
            src_ref=point_ref,
            dst_ref=points.at[step],
            send_sem=point_send.at[step],
            recv_sem=point_recv.at[step],
            device_id={"sub": (sub_at + step) % subs},
            device_id_type=MESH,
        )

    halo_start(0)
    for step in range(1, subs):
        point_copy(step).start()
    tell(0)
    base_load.wait()

    def features(ref, at, xyz, own):
        one, two, three = split3(xyz)
        square = xyz[0:1] * xyz[0:1] + xyz[1:2] * xyz[1:2] + xyz[2:3] * xyz[2:3]
        pieces = [one, one, two, two, one, three] if own else [one, two, one, two, three, one]
        for slot, piece in enumerate(pieces):
            ref[3 * slot : 3 * slot + 3, at] = piece if own else -2.0 * piece
        parts = split3(square)
        for slot in range(3):
            ones = jnp.ones_like(square)
            ref[18 + slot : 19 + slot, at] = parts[slot] if own else ones
            ref[21 + slot : 22 + slot, at] = ones if own else parts[slot]

    inverse_radius = 1.0 / support_radius
    features(base_feat, slice(None), (base_ref[...] - 0.5) * inverse_radius, False)

    def build_kernel(step):
        xyz = point_ref[...] if step == 0 else points[step]
        features(cell_feat, slice(None), (xyz - 0.5) * inverse_radius, True)

        def tile(index, carry):
            source = pl.ds(pl.multiple_of(index * TILE, TILE), TILE)
            target = pl.ds(pl.multiple_of(step * cell_count + index * TILE, TILE), TILE)
            mine = cell_feat[:, source].T.astype(jnp.bfloat16)
            for left in range(0, base_own, TILE):
                other = base_feat[:, left : left + TILE].astype(jnp.bfloat16)
                squared = jnp.dot(mine, other, preferred_element_type=jnp.float32)
                squared = jnp.maximum(squared, 1e-20)
                ratio = squared * lax.rsqrt(squared)
                inside = jnp.maximum(1.0 - ratio, 0.0)
                inside = inside * inside
                value = inside * inside * (4.0 * ratio + 1.0)
                hi, lo = split2(value)
                k_hi[target, left : left + TILE] = hi
                k_lo[target, left : left + TILE] = lo
            return carry

        lax.fori_loop(0, cell_count // TILE, tile, 0)

    def relax(sweep):
        stride = ROWS // nodes_here
        for start in range(win.shape[0]):
            for comp in range(5):
                at = start * nodes_here
                win[start, comp] = wide[sweep, comp, at : at + ROWS, :]

        def face_step(face, coupled):
            beside = [[] for _ in range(5)]
            for piece in range(rows // ROWS):
                span = slice(piece * ROWS, (piece + 1) * ROWS)
                rel, lane = rel_ref[face, span, :], lane_ref[face, span, :]
                found = [jnp.zeros((ROWS, LANES), jnp.float32)] * 5
                for chunk in range(2 * blocks + 1):
                    match = rel == chunk
                    for comp in range(5):
                        taken = jnp.take_along_axis(
                            win[chunk + stride * piece, comp], lane, axis=1
                        )
                        found[comp] = jnp.where(match, taken, found[comp])
                for comp in range(5):
                    beside[comp].append(found[comp])
            beside = [jnp.concatenate(part, axis=0) for part in beside]
            coupled = list(coupled)
            for a in range(5):
                for b in range(5):
                    block = off_ref[face, 5 * a + b].astype(jnp.float32)
                    coupled[a] = coupled[a] + block * beside[b]
            return tuple(coupled)

        zero = jnp.zeros((rows, LANES), jnp.float32)
        coupled = lax.fori_loop(0, off_ref.shape[0], face_step, (zero,) * 5)
        if sweep == 0:
            rhs_load.wait()
            inv_load.wait()
        rest = [rhs_ref[b] - coupled[b] for b in range(5)]
        result = []
        for a in range(5):
            total = inv_ref[5 * a] * rest[0]
            for b in range(1, 5):
                total = total + inv_ref[5 * a + b] * rest[b]
            result.append(total)
        return result

    build_kernel(0)
    halo_wait(0)
    off_load.wait()
    first = relax(0)
    for a in range(5):
        wide[1, a, rows : 2 * rows, :] = first[a]
    halo_start(1)
    if cells > 2:
        hear(0)
        tell(1)
    for step in range(1, subs):
        point_copy(step).wait_recv()
        build_kernel(step)
    halo_wait(1)
    adjoint = relax(1)
    for a in range(5):
        out_ref[a] = adjoint[a]

    sens_load.wait()
    for k in range(3):
        total = adjoint[0] * sens_ref[k].astype(jnp.float32)
        for a in range(1, 5):
            total = total + adjoint[a] * sens_ref[3 * a + k].astype(jnp.float32)
        sens_rows[k] = total
    for k in range(3):
        total = weight_ref[0] * sens_rows[k, pl.ds(0, blocks, stride=nodes_here), :]
        for n in range(1, nodes_here):
            total = total + weight_ref[n] * sens_rows[k, pl.ds(n, blocks, stride=nodes_here), :]
        sens_slots[team, k] = total

    def sens_copy(step):
        return pltpu.make_async_remote_copy(
            src_ref=sens_slots.at[team],
            dst_ref=sens_slots.at[team],
            send_sem=sens_send.at[step],
            recv_sem=sens_recv.at[team],
            device_id=member((team + step) % crew),
            device_id_type=MESH,
        )

    def sens_arrival(step):
        slot = (team + step) % crew
        return pltpu.make_async_remote_copy(
            src_ref=sens_slots.at[slot],
            dst_ref=sens_slots.at[slot],
            send_sem=sens_send.at[step],
            recv_sem=sens_recv.at[slot],
            device_id=member((team + step) % crew),
            device_id_type=MESH,
        )

    for step in range(1, crew):
        sens_copy(step).start()
    for stage in range(2, cells - 1):
        hear(stage - 1)
        tell(stage)
    sens_mat[...] = jnp.zeros_like(sens_mat)
    loads[8].wait()
    loads[9].wait()
    lax.fori_loop(0, base_own // LANES, build_lattice, 0)
    for step in range(1, crew):
        sens_arrival(step).wait_recv()
    for step in range(subs):
        whose = (sub_at - step + subs) % subs
        for k in range(3):
            total = sens_slots[whose, k]
            for n in range(1, nodes):
                total = total + sens_slots[n * subs + whose, k]
            hi = total.astype(jnp.bfloat16).astype(jnp.float32)
            lo = total - hi
            for block in range(blocks):
                at = step * cell_count + block * LANES
                sens_mat[k : k + 1, at : at + LANES] = hi[block : block + 1, :]
                sens_mat[ROWS + k : ROWS + k + 1, at : at + LANES] = lo[block : block + 1, :]

    left = sens_mat[...].astype(jnp.bfloat16)
    product = jnp.dot(left, k_hi[...], preferred_element_type=jnp.float32)
    product = product + jnp.dot(left, k_lo[...], preferred_element_type=jnp.float32)
    base_grad = (product[0:ROWS] + product[ROWS:]) * scale
    hi = base_grad.astype(jnp.bfloat16).astype(jnp.float32)
    left = jnp.concatenate([hi, base_grad - hi], axis=0).astype(jnp.bfloat16)
    contract = (((1,), (1,)), ((), ()))
    product = lax.dot_general(left, l_hi[...], contract, preferred_element_type=jnp.float32)
    product = product + lax.dot_general(
        left, l_lo[...], contract, preferred_element_type=jnp.float32
    )
    own = product[0:ROWS] + product[ROWS:]
    for block in range(FFD // LANES):
        grad_slots[me, 3 * block : 3 * block + 3, :] = own[
            0:3, block * LANES : (block + 1) * LANES
        ]

    def grad_copy(step, slot):
        return pltpu.make_async_remote_copy(
            src_ref=grad_slots.at[slot],
            dst_ref=grad_slots.at[slot],
            send_sem=grad_send.at[step],
            recv_sem=grad_recv.at[slot],
            device_id=anyone((me + step) % everyone),
            device_id_type=MESH,
        )

    if cells > 1:
        hear(cells - 2)
    for step in range(1, everyone):
        grad_copy(step, me).start()
    halo_sent(0)
    halo_sent(1)
    for step in range(1, subs):
        point_copy(step).wait_send()
    for step in range(1, crew):
        sens_copy(step).wait_send()
    for step in range(1, everyone):
        grad_copy(step, (me + step) % everyone).wait_recv()
    total = grad_slots[0]
    for slot in range(1, everyone):
        total = total + grad_slots[slot]
    for block in range(FFD // LANES):
        grad_ref[:, block * LANES : (block + 1) * LANES] = total[3 * block : 3 * block + 3, :]
    for step in range(1, everyone):
        grad_copy(step, me).wait_send()


def finish(adjoint_in, control_in, adjoint_out, control_out):
    adjoint_out[...] = adjoint_in[...]
    control_out[...] = control_in[...]


def to_rows(array):
    array = jnp.moveaxis(array, 0, -2)
    lead, (nodes, cells) = array.shape[:-2], array.shape[-2:]
    array = array.reshape(lead + (nodes, cells // LANES, LANES))
    array = jnp.swapaxes(array, -3, -2)
    return array.reshape(lead + (nodes * cells // LANES, LANES))


def from_rows(array, nodes):
    lead, rows = array.shape[:-2], array.shape[-2]
    array = array.reshape(lead + (rows // nodes, nodes, LANES))
    array = jnp.swapaxes(array, -3, -2).reshape(lead + (nodes, rows // nodes * LANES))
    return jnp.moveaxis(array, -2, 0)


def body(
    adjoint_start,
    adjoint_rhs,
    off_blocks,
    diag_inverse,
    neighbours,
    node_weights,
    sens_blocks,
    cell_points,
    base_points,
    ffd_index,
    ffd_weight,
):
    nodes_here, _, cell_count = adjoint_start.shape
    faces = off_blocks.shape[1]
    cells, subs, nodes = (lax.axis_size(a) for a in ("cells", "sub", "nodes"))
    crew = nodes * subs
    everyone = cells * crew
    blocks = cell_count // LANES
    rows = blocks * nodes_here
    base_own = base_points.shape[1] // crew
    windows = 2 * blocks + 1 + (rows // ROWS - 1) * (ROWS // nodes_here)
    scale = 1.0 / float(cell_count * cells * subs) ** 0.5
    vmem = pl.BlockSpec(memory_space=pltpu.VMEM)
    hbm = pl.BlockSpec(memory_space=pltpu.HBM)
    f32, bf16 = jnp.float32, jnp.bfloat16
    dma = pltpu.SemaphoreType.DMA
    off_rows, inv_rows = to_rows(off_blocks), to_rows(diag_inverse)
    sens_cells = to_rows(sens_blocks)
    adjoint, control = pl.pallas_call(
        functools.partial(kernel, scale),
        out_shape=(
            jax.ShapeDtypeStruct((5, rows, LANES), f32),
            jax.ShapeDtypeStruct((3, FFD), f32),
        ),
        in_specs=[pl.BlockSpec(memory_space=pltpu.SMEM)] + [hbm] * 10,
        out_specs=(vmem, vmem),
        scratch_shapes=[
            pltpu.VMEM(cell_points.shape, f32),
            pltpu.VMEM(neighbours.shape, jnp.int32),
            pltpu.VMEM((3, base_own), f32),
            pltpu.VMEM(off_rows.shape, bf16),
            pltpu.VMEM((5, rows, LANES), f32),
            pltpu.VMEM(inv_rows.shape, f32),
            pltpu.VMEM(sens_cells.shape, bf16),
            pltpu.VMEM((ffd_index.shape[1], base_own), jnp.int32),
            pltpu.VMEM((ffd_index.shape[1], base_own), f32),
            pltpu.VMEM((SWEEPS, 5, 3 * rows, LANES), f32),
            pltpu.VMEM((windows, 5, ROWS, LANES), f32),
            pltpu.VMEM((faces, rows, LANES), jnp.int32),
            pltpu.VMEM((faces, rows, LANES), jnp.int32),
            pltpu.VMEM((subs, 3, cell_count), f32),
            pltpu.VMEM((24, cell_count), f32),
            pltpu.VMEM((24, base_own), f32),
            pltpu.VMEM((subs * cell_count, base_own), bf16),
            pltpu.VMEM((subs * cell_count, base_own), bf16),
            pltpu.VMEM((FFD, base_own), bf16),
            pltpu.VMEM((FFD, base_own), bf16),
            pltpu.VMEM((3, rows, LANES), f32),
            pltpu.VMEM((crew, 3, blocks, LANES), f32),
            pltpu.VMEM((2 * ROWS, subs * cell_count), f32),
            pltpu.VMEM((everyone, 3 * FFD // LANES, LANES), f32),
            dma((10,)),
            dma((SWEEPS, 2)),
            dma((SWEEPS, 2)),
            dma((subs,)),
            dma((subs,)),
            dma((crew,)),
            dma((crew,)),
            dma((everyone,)),
            dma((everyone,)),
            pltpu.SemaphoreType.REGULAR((max(cells - 1, 1), 2)),
        ],
        compiler_params=pltpu.CompilerParams(
            collective_id=0, has_side_effects=True, vmem_limit_bytes=16 * 1024 * 1024
        ),
    )(
        node_weights,
        *(pltpu.with_memory_space_constraint(array, pltpu.HBM) for array in (
            to_rows(adjoint_start),
            cell_points,
            neighbours,
            base_points,
            off_rows,
            to_rows(adjoint_rhs),
            inv_rows,
            sens_cells,
            ffd_index.T,
            ffd_weight.T,
        ))
    )
    adjoint, control = pl.pallas_call(
        finish,
        out_shape=(
            jax.ShapeDtypeStruct((5, rows, LANES), f32),
            jax.ShapeDtypeStruct((3, FFD), f32),
        ),
        in_specs=[vmem] * 2,
        out_specs=(vmem, vmem),
        compiler_params=pltpu.CompilerParams(vmem_limit_bytes=1024 * 1024),
    )(adjoint, control)
    return from_rows(adjoint, nodes_here), control


def solution(mesh):
    return jax.shard_map(
        body,
        mesh=mesh,
        in_specs=(
            P("nodes", None, ("groups", "cells", "sub")),
            P("nodes", None, ("groups", "cells", "sub")),
            P("nodes", None, None, ("groups", "cells", "sub")),
            P("nodes", None, ("groups", "cells", "sub")),
            P(None, ("cells", "sub")),
            P("nodes"),
            P("nodes", None, ("groups", "cells", "sub")),
            P(None, ("cells", "sub")),
            P(),
            P(),
            P(),
        ),
        out_specs=(P("nodes", None, ("groups", "cells", "sub")), P("groups", None)),
        check_vma=False,
    )
```

profile of v0, /device:TPU:0, one launch (start us, length us, event | category | flops | bytes accessed | tf_op | source)
XLA Modules:
  0.0 25.3 jit_solution(16172453545033344468)
XLA Ops:
  0.6 0.0 copy-start
  0.6 0.6 %copy-done = f32[2]{0:T(128)S(1)} copy-done((f32[2]{0:T(128)S(1)}, f32[2]{0:T(128)}, u32[]{:S(2)}) %copy-start) | copy-done | bytes 32
  1.3 23.3 %shard_map.122 = (f32[5,16,128]{2,1,0:T(8,128)S(1)}, f32[3,512]{1,0:T(4,128)S(1)}) custom-call(f32[2]{0:T(128)S(1)} %copy-done, f32[5,16,128]{2,1,0:T(8,128)} %bitcast.49, f32[3,1024]{1,0:T(4,128)} %point_hbm.1, s32[6,1024]{1,0:T(8,128)} %nb_hbm.1, f32[3,4096]{1,0:T(4,128)} %base_hbm.1, bf16[6,25,16,128]{3,2,1,0:T(8,128)(2,1)} %bitcast.44, ...), custom_call_target="tpu_custom_call" | custom-call | tf_op jit(solution)/shard_map/pallas_call | solution.py:508
  24.6 0.6 %shard_map.123 = (f32[5,16,128]{2,1,0:T(8,128)}, f32[3,512]{1,0:T(4,128)}) custom-call(f32[5,16,128]{2,1,0:T(8,128)S(1)} %get-tuple-element.6.adjoint_in, f32[3,512]{1,0:T(4,128)S(1)} %get-tuple-element.7.control_in), custom_call_target="tpu_custom_call" | custom-call | tf_op jit(solution)/shard_map/pallas_call | solution.py:570
Async XLA Ops:
  0.6 0.7 %copy-start = (f32[2]{0:T(128)S(1)}, f32[2]{0:T(128)}, u32[]{:S(2)}) copy-start(f32[2]{0:T(128)} %weight_ref.1) | copy-start | bytes 28
where the time goes:
time: 25.4 us; the launch traced here: 25.3 us
  Pallas kernels  24 us (94%)
  local copies, waits for them, and re-layouts  0.65 us (3%)
  between operations  0.65 us (3%)
    pallas_call x1, Pallas kernels, body(): pl.pallas_call(functools.partial(kernel, scale), out_shape=(jax.ShapeDtyp...  23.3 us
    unnamed x2, local copies, waits for them, and re-layouts  0.65 us
    pallas_call x1, Pallas kernels, body(): pl.pallas_call(finish, out_shape=(jax.ShapeDtypeStruct((5, rows, LANES),...  0.62 us

commit v1 on v0

v1 whole, which is shorter than its diff:
```python
import functools

import jax
import jax.numpy as jnp
from jax import lax
from jax.experimental import pallas as pl
from jax.experimental.pallas import tpu as pltpu
from jax.sharding import PartitionSpec as P

SWEEPS = 2
FFD = 512
LANES = 128
ROWS = 8
PIECE = 64

support_radius = 0.3
MESH = pl.DeviceIdType.MESH


def split2(x):
    hi = x.astype(jnp.bfloat16)
    return hi, (x - hi.astype(jnp.float32)).astype(jnp.bfloat16)


def split3(x):
    one = x.astype(jnp.bfloat16).astype(jnp.float32)
    two = (x - one).astype(jnp.bfloat16).astype(jnp.float32)
    return one, two, (x - one) - two


def kernel(
    scale,
    weight_hbm,
    adj_hbm,
    point_hbm,
    nb_hbm,
    base_hbm,
    off_hbm,
    rhs_hbm,
    inv_hbm,
    sens_hbm,
    ffd_index_hbm,
    ffd_weight_hbm,
    out_ref,
    grad_ref,
    weight_ref,
    point_ref,
    nb_ref,
    base_ref,
    off_ref,
    rhs_ref,
    inv_ref,
    sens_ref,
    ffd_index_ref,
    ffd_weight_ref,
    wide,
    rel_ref,
    lane_ref,
    points,
    cell_rows,
    cell_feat,
    base_feat,
    k_hi,
    k_lo,
    l_hi,
    l_lo,
    sens_rows,
    sens_slots,
    sens_mat,
    grad_slots,
    load_sem,
    halo_send,
    halo_recv,
    point_send,
    point_recv,
    sens_send,
    sens_recv,
    grad_send,
    grad_recv,
    known,
):
    cells, subs, nodes = (lax.axis_size(a) for a in ("cells", "sub", "nodes"))
    cell_at, sub_at, node_at = (lax.axis_index(a) for a in ("cells", "sub", "nodes"))
    here, places = cell_at * subs + sub_at, cells * subs
    team, crew = node_at * subs + sub_at, nodes * subs
    me, everyone = cell_at * crew + team, cells * crew
    nodes_here = weight_ref.shape[0]
    rows = adj_hbm.shape[1]
    blocks = rows // nodes_here
    cell_count = blocks * LANES
    base_own = base_ref.shape[1]
    panels = base_own // LANES

    def member(index):
        return {"nodes": index // subs, "sub": index % subs}

    def anyone(index):
        return dict(member(index % crew), cells=index // crew)

    lower, upper = cell_at > 0, cell_at < cells - 1
    below, above = cell_at - 1, cell_at + 1
    beside_count = lower.astype(jnp.int32) + upper.astype(jnp.int32)

    base_start = pl.multiple_of(team * base_own, LANES)
    share = pl.ds(base_start, base_own)
    sources = (
        (0, adj_hbm, wide.at[0, :, pl.ds(rows, rows), :]),
        (1, point_hbm, point_ref),
        (2, base_hbm.at[:, share], base_ref),
        (3, nb_hbm, nb_ref),
        (4, off_hbm, off_ref),
        (5, rhs_hbm, rhs_ref),
        (5, inv_hbm, inv_ref),
        (6, sens_hbm, sens_ref),
        (7, ffd_index_hbm.at[:, share], ffd_index_ref),
        (7, ffd_weight_hbm.at[:, share], ffd_weight_ref),
        (8, weight_hbm, weight_ref),
    )
    for group, source, target in sources:
        pltpu.make_async_copy(source, target, load_sem.at[group]).start()

    def arrive(size, sem):
        pltpu.make_async_copy(size, size, sem).wait()

    sizes = [source[2] for source in sources if source[0] not in (5, 7)]
    sizes.insert(5, wide)
    sizes.insert(7, cell_feat.at[0 : 2 * ffd_index_ref.shape[0], 0:base_own])

    def load_wait(*groups):
        for group in groups:
            arrive(sizes[group], load_sem.at[group])

    barrier = pltpu.get_barrier_semaphore()

    def greet(device):
        pl.semaphore_signal(barrier, inc=1, device_id=device, device_id_type=MESH)

    greeted = crew - 1
    for step in range(1, crew):
        greet(member((team + step) % crew))
    greetings = [(lower, {"cells": below}), (upper, {"cells": above})]
    if subs > 1:
        first, last = sub_at == 0, sub_at == subs - 1
        greetings.append((jnp.logical_and(lower, first), {"cells": below, "sub": subs - 1}))
        greetings.append((jnp.logical_and(upper, last), {"cells": above, "sub": 0}))
    for exists, device in greetings:
        pl.when(exists)(functools.partial(greet, device))
        greeted = greeted + exists.astype(jnp.int32)

    def tell(stage):
        for exists, other in ((upper, above), (lower, below)):

            @pl.when(exists)
            def _():
                pl.semaphore_signal(
                    known.at[stage],
                    inc=1,
                    device_id={"cells": other},
                    device_id_type=MESH,
                )

    def hear(stage):
        pl.semaphore_wait(known.at[stage], beside_count)

    @pl.when(here == 0)
    def _():
        wide[:, :, 0:rows, :] = jnp.zeros((SWEEPS, 5, rows, LANES), jnp.float32)

    @pl.when(here == places - 1)
    def _():
        wide[:, :, 2 * rows : 3 * rows, :] = jnp.zeros((SWEEPS, 5, rows, LANES), jnp.float32)

    def halo(sweep, side):
        other = here + 1 if side == 0 else here - 1
        start = 0 if side == 0 else 2 * rows
        return pltpu.make_async_remote_copy(
            src_ref=wide.at[sweep, :, pl.ds(rows, rows), :],
            dst_ref=wide.at[sweep, :, pl.ds(start, rows), :],
            send_sem=halo_send.at[side],
            recv_sem=halo_recv.at[sweep, side],
            device_id={"cells": other // subs, "sub": other % subs},
            device_id_type=MESH,
        )

    def halo_start(sweep):
        @pl.when(here < places - 1)
        def _():
            halo(sweep, 0).start()

        @pl.when(here > 0)
        def _():
            halo(sweep, 1).start()

    def halo_wait(sweep):
        @pl.when(here > 0)
        def _():
            halo(sweep, 0).wait_recv()

        @pl.when(here < places - 1)
        def _():
            halo(sweep, 1).wait_recv()

    def halo_sent():
        both = wide.at[:, :, pl.ds(rows, rows), :]

        @pl.when(here < places - 1)
        def _():
            arrive(both, halo_send.at[0])

        @pl.when(here > 0)
        def _():
            arrive(both, halo_send.at[1])

    def point_copy(step):
        return pltpu.make_async_remote_copy(
            src_ref=point_ref,
            dst_ref=points.at[step],
            send_sem=point_send.at[step],
            recv_sem=point_recv.at[step],
            device_id={"sub": (sub_at + step) % subs},
            device_id_type=MESH,
        )

    load_wait(0, 1)
    pl.semaphore_wait(barrier, greeted)
    halo_start(0)
    for step in range(1, subs):
        point_copy(step).start()
    tell(0)

    load_wait(2, 3)
    first_cell = here * cell_count
    for face in range(nb_ref.shape[0]):
        for block in range(blocks):
            entry = nb_ref[face : face + 1, block * LANES : (block + 1) * LANES]
            local = entry - first_cell + cell_count
            chunk = jnp.where(entry >= 0, (local >> 7) - block, -1)
            span = pl.ds(block * nodes_here, nodes_here)
            rel_ref[face, span, :] = jnp.broadcast_to(chunk, (nodes_here, LANES))
            lane_ref[face, span, :] = jnp.broadcast_to(local & (LANES - 1), (nodes_here, LANES))

    def features(xyz, own):
        one, two, three = split3(xyz)
        square = xyz[0:1] * xyz[0:1] + xyz[1:2] * xyz[1:2] + xyz[2:3] * xyz[2:3]
        pieces = [one, one, two, two, one, three] if own else [one, two, one, two, three, one]
        parts = split3(square)
        ones = jnp.ones_like(square)
        for slot, piece in enumerate(pieces):
            cell_feat[3 * slot : 3 * slot + 3, 0 : xyz.shape[1]] = piece if own else -2.0 * piece
        for slot in range(3):
            cell_feat[18 + slot : 19 + slot, 0 : xyz.shape[1]] = parts[slot] if own else ones
            cell_feat[21 + slot : 22 + slot, 0 : xyz.shape[1]] = ones if own else parts[slot]

    stretch = 4.0 / support_radius
    features((base_ref[...] - 0.5) * stretch, False)
    base_feat[...] = cell_feat[:, 0:base_own].astype(jnp.bfloat16)

    def build_kernel(step):
        xyz = point_ref[...] if step == 0 else points[step]
        features((xyz - 0.5) * stretch, True)
        cell_rows[...] = cell_feat[:, 0:cell_count].T.astype(jnp.bfloat16)
        width = 2 * LANES
        for left in range(0, base_own, width):
            other = base_feat[:, left : left + width]
            for top in range(0, cell_count, PIECE):
                mine = cell_rows[top : top + PIECE, :]
                target = slice(step * cell_count + top, step * cell_count + top + PIECE)
                squared = jnp.dot(mine, other, preferred_element_type=jnp.float32)
                squared = jnp.maximum(squared, 1e-20)
                ratio = squared * lax.rsqrt(squared)
                inside = jnp.maximum(4.0 - ratio, 0.0)
                fourth = inside * inside
                value = (fourth * fourth) * (5.0 - inside)
                for side in range(2):
                    hi, lo = split2(value[:, side * LANES : (side + 1) * LANES])
                    k_hi[left // LANES + side, target, :] = hi
                    k_lo[left // LANES + side, target, :] = lo

    def build_lattice(panel, carry):
        at = pl.ds(pl.multiple_of(panel * LANES, LANES), LANES)
        index, weight = ffd_index_ref[:, at], ffd_weight_ref[:, at]
        slots = index.shape[0]
        slot = lax.broadcasted_iota(jnp.int32, index.shape, 0)
        total, repeat = weight, jnp.zeros(index.shape, jnp.int32)
        for turn in range(1, slots):
            same = pltpu.roll(index, turn, 0) == index
            total = total + jnp.where(same, pltpu.roll(weight, turn, 0), 0.0)
            repeat = jnp.where(jnp.logical_and(same, slot >= turn), 1, repeat)
        index = jnp.where(repeat == 1, -1, index)
        hi = total.astype(jnp.bfloat16).astype(jnp.float32)
        lo = total - hi
        tall = (2 * ROWS, LANES)

        def spread(value, kind):
            return [jnp.broadcast_to(value[s : s + 1], tall).astype(kind) for s in range(slots)]

        index, hi, lo = spread(index, jnp.int16), spread(hi, jnp.bfloat16), spread(lo, jnp.bfloat16)
        row = lax.broadcasted_iota(jnp.int32, tall, 0).astype(jnp.int16)
        for top in range(0, FFD, 2 * ROWS):
            found_hi = found_lo = jnp.zeros(tall, jnp.bfloat16)
            here_row = row + jnp.int16(top)
            for s in range(slots):
                match = index[s] == here_row
                found_hi = jnp.where(match, hi[s], found_hi)
                found_lo = jnp.where(match, lo[s], found_lo)
            l_hi[panel, top : top + 2 * ROWS, :] = found_hi
            l_lo[panel, top : top + 2 * ROWS, :] = found_lo
        return carry

    def relax(sweep):
        pieces, stride = rows // ROWS, ROWS // nodes_here
        zero = jnp.zeros((ROWS, LANES), jnp.float32)
        coupled = [[zero] * 5 for _ in range(pieces)]
        for face in range(off_ref.shape[0]):
            for piece in range(pieces):
                span = slice(piece * ROWS, (piece + 1) * ROWS)
                rel, lane = rel_ref[face, span, :], lane_ref[face, span, :]
                found = [zero] * 5
                for chunk in range(2 * blocks + 1):
                    match = rel == chunk
                    at = (chunk + stride * piece) * nodes_here
                    for comp in range(5):
                        window = wide[sweep, comp, at : at + ROWS, :]
                        taken = jnp.take_along_axis(window, lane, axis=1)
                        found[comp] = jnp.where(match, taken, found[comp])
                for a in range(5):
                    for b in range(5):
                        block = off_ref[face, 5 * a + b, span].astype(jnp.float32)
                        coupled[piece][a] = coupled[piece][a] + block * found[b]
        result = []
        for piece in range(pieces):
            span = slice(piece * ROWS, (piece + 1) * ROWS)
            rest = [rhs_ref[b, span] - coupled[piece][b] for b in range(5)]
            totals = []
            for a in range(5):
                total = inv_ref[5 * a, span] * rest[0]
                for b in range(1, 5):
                    total = total + inv_ref[5 * a + b, span] * rest[b]
                totals.append(total)
            result.append(totals)
        return result

    build_kernel(0)
    load_wait(4, 5)
    halo_wait(0)
    result = relax(0)
    for piece, totals in enumerate(result):
        for a in range(5):
            wide[1, a, rows + piece * ROWS : rows + (piece + 1) * ROWS, :] = totals[a]
    halo_start(1)
    if cells > 2:
        hear(0)
        tell(1)
    for step in range(1, subs):
        point_copy(step).wait_recv()
        build_kernel(step)
    load_wait(6, 7, 8)
    halo_wait(1)
    result = relax(1)
    for piece, totals in enumerate(result):
        span = slice(piece * ROWS, (piece + 1) * ROWS)
        for k in range(3):
            total = totals[0] * sens_ref[k, span].astype(jnp.float32)
            for a in range(1, 5):
                total = total + totals[a] * sens_ref[3 * a + k, span].astype(jnp.float32)
            sens_rows[k, span, :] = total
    for k in range(3):
        total = weight_ref[0] * sens_rows[k, pl.ds(0, blocks, stride=nodes_here), :]
        for n in range(1, nodes_here):
            total = total + weight_ref[n] * sens_rows[k, pl.ds(n, blocks, stride=nodes_here), :]
        sens_slots[team, k] = total

    def sens_copy(step):
        return pltpu.make_async_remote_copy(
            src_ref=sens_slots.at[team],
            dst_ref=sens_slots.at[team],
            send_sem=sens_send,
            recv_sem=sens_recv,
            device_id=member((team + step) % crew),
            device_id_type=MESH,
        )

    for step in range(1, crew):
        sens_copy(step).start()
    for piece, totals in enumerate(result):
        for a in range(5):
            out_ref[a, piece * ROWS : (piece + 1) * ROWS, :] = totals[a]
    for stage in range(2, cells - 1):
        hear(stage - 1)
        tell(stage)
    sens_mat[...] = jnp.zeros_like(sens_mat)
    lax.fori_loop(0, panels, build_lattice, 0)
    arrive(sens_slots.at[pl.ds(0, crew - 1)], sens_recv)
    for step in range(subs):
        whose = (sub_at - step + subs) % subs
        for k in range(3):
            total = sens_slots[whose, k]
            for n in range(1, nodes):
                total = total + sens_slots[n * subs + whose, k]
            hi = total.astype(jnp.bfloat16).astype(jnp.float32)
            lo = total - hi
            for block in range(blocks):
                at = step * cell_count + block * LANES
                sens_mat[k : k + 1, at : at + LANES] = hi[block : block + 1, :]
                sens_mat[ROWS + k : ROWS + k + 1, at : at + LANES] = lo[block : block + 1, :]

    left = sens_mat[...].astype(jnp.bfloat16)
    contract = (((1,), (1,)), ((), ()))
    own = jnp.zeros((2 * ROWS, FFD), jnp.float32)
    grads = []
    for pair in range(0, panels, 2):
        product = jnp.zeros((2 * ROWS, 2 * LANES), jnp.float32)
        for table in (k_hi, k_lo):
            both = jnp.concatenate([table[pair], table[pair + 1]], axis=1)
            product = product + jnp.dot(left, both, preferred_element_type=jnp.float32)
        grads.append((product[0:ROWS] + product[ROWS:]) * scale)
    for pair in range(0, panels, 2):
        base_grad = grads[pair // 2]
        hi = base_grad.astype(jnp.bfloat16).astype(jnp.float32)
        sides = jnp.concatenate([hi, base_grad - hi], axis=0).astype(jnp.bfloat16)
        for table in (l_hi, l_lo):
            both = jnp.concatenate([table[pair], table[pair + 1]], axis=1)
            own = own + lax.dot_general(sides, both, contract, preferred_element_type=jnp.float32)
    own = own[0:ROWS] + own[ROWS:]
    for block in range(FFD // LANES):
        grad_slots[me, 3 * block : 3 * block + 3, :] = own[
            0:3, block * LANES : (block + 1) * LANES
        ]

    def grad_copy(step):
        return pltpu.make_async_remote_copy(
            src_ref=grad_slots.at[me],
            dst_ref=grad_slots.at[me],
            send_sem=grad_send,
            recv_sem=grad_recv,
            device_id=anyone((me + step) % everyone),
            device_id_type=MESH,
        )

    if cells > 1:
        hear(cells - 2)
    for step in range(1, everyone):
        grad_copy(step).start()
    halo_sent()
    for step in range(1, subs):
        point_copy(step).wait_send()
    arrive(sens_slots.at[pl.ds(0, crew - 1)], sens_send)
    others = grad_slots.at[pl.ds(0, everyone - 1)]
    arrive(others, grad_send)
    arrive(others, grad_recv)
    total = grad_slots[0]
    for slot in range(1, everyone):
        total = total + grad_slots[slot]
    for block in range(FFD // LANES):
        grad_ref[:, block * LANES : (block + 1) * LANES] = total[3 * block : 3 * block + 3, :]


def finish(adjoint_in, control_in, adjoint_out, control_out):
    adjoint_out[...] = adjoint_in[...]
    control_out[...] = control_in[...]


def to_rows(array):
    array = jnp.moveaxis(array, 0, -2)
    lead, (nodes, cells) = array.shape[:-2], array.shape[-2:]
    array = array.reshape(lead + (nodes, cells // LANES, LANES))
    array = jnp.swapaxes(array, -3, -2)
    return array.reshape(lead + (nodes * cells // LANES, LANES))


def from_rows(array, nodes):
    lead, rows = array.shape[:-2], array.shape[-2]
    array = array.reshape(lead + (rows // nodes, nodes, LANES))
    array = jnp.swapaxes(array, -3, -2).reshape(lead + (nodes, rows // nodes * LANES))
    return jnp.moveaxis(array, -2, 0)


def body(
    adjoint_start,
    adjoint_rhs,
    off_blocks,
    diag_inverse,
    neighbours,
    node_weights,
    sens_blocks,
    cell_points,
    base_points,
    ffd_index,
    ffd_weight,
):
    nodes_here, _, cell_count = adjoint_start.shape
    faces = off_blocks.shape[1]
    cells, subs, nodes = (lax.axis_size(a) for a in ("cells", "sub", "nodes"))
    crew = nodes * subs
    everyone = cells * crew
    blocks = cell_count // LANES
    rows = blocks * nodes_here
    base_own = base_points.shape[1] // crew
    panels = base_own // LANES
    scale = 1.0 / 256.0 / float(cell_count * cells * subs) ** 0.5
    vmem = pl.BlockSpec(memory_space=pltpu.VMEM)
    hbm = pl.BlockSpec(memory_space=pltpu.HBM)
    f32, bf16 = jnp.float32, jnp.bfloat16
    dma = pltpu.SemaphoreType.DMA
    off_rows, inv_rows = to_rows(off_blocks), to_rows(diag_inverse)
    sens_cells = to_rows(sens_blocks)
    adjoint, control = pl.pallas_call(
        functools.partial(kernel, scale),
        out_shape=(
            jax.ShapeDtypeStruct((5, rows, LANES), f32),
            jax.ShapeDtypeStruct((3, FFD), f32),
        ),
        in_specs=[hbm] * 11,
        out_specs=(vmem, vmem),
        scratch_shapes=[
            pltpu.SMEM(node_weights.shape, f32),
            pltpu.VMEM(cell_points.shape, f32),
            pltpu.VMEM(neighbours.shape, jnp.int32),
            pltpu.VMEM((3, base_own), f32),
            pltpu.VMEM(off_rows.shape, bf16),
            pltpu.VMEM((5, rows, LANES), f32),
            pltpu.VMEM(inv_rows.shape, f32),
            pltpu.VMEM(sens_cells.shape, bf16),
            pltpu.VMEM((ffd_index.shape[1], base_own), jnp.int32),
            pltpu.VMEM((ffd_index.shape[1], base_own), f32),
            pltpu.VMEM((SWEEPS, 5, 3 * rows, LANES), f32),
            pltpu.VMEM((faces, rows, LANES), jnp.int32),
            pltpu.VMEM((faces, rows, LANES), jnp.int32),
            pltpu.VMEM((subs, 3, cell_count), f32),
            pltpu.VMEM((cell_count, 24), bf16),
            pltpu.VMEM((24, max(cell_count, base_own)), f32),
            pltpu.VMEM((24, base_own), bf16),
            pltpu.VMEM((panels, subs * cell_count, LANES), bf16),
            pltpu.VMEM((panels, subs * cell_count, LANES), bf16),
            pltpu.VMEM((panels, FFD, LANES), bf16),
            pltpu.VMEM((panels, FFD, LANES), bf16),
            pltpu.VMEM((3, rows, LANES), f32),
            pltpu.VMEM((crew, 3, blocks, LANES), f32),
            pltpu.VMEM((2 * ROWS, subs * cell_count), f32),
            pltpu.VMEM((everyone, 3 * FFD // LANES, LANES), f32),
            dma((9,)),
            dma((2,)),
            dma((SWEEPS, 2)),
            dma((subs,)),
            dma((subs,)),
            dma,
            dma,
            dma,
            dma,
            pltpu.SemaphoreType.REGULAR((max(cells - 1, 1),)),
        ],
        compiler_params=pltpu.CompilerParams(
            collective_id=0, has_side_effects=True, vmem_limit_bytes=16 * 1024 * 1024
        ),
    )(
        *(pltpu.with_memory_space_constraint(array, pltpu.HBM) for array in (
            node_weights,
            to_rows(adjoint_start),
            cell_points,
            neighbours,
            base_points,
            off_rows,
            to_rows(adjoint_rhs),
            inv_rows,
            sens_cells,
            ffd_index.T,
            ffd_weight.T,
        ))
    )
    adjoint, control = pl.pallas_call(
        finish,
        out_shape=(
            jax.ShapeDtypeStruct((5, rows, LANES), f32),
            jax.ShapeDtypeStruct((3, FFD), f32),
        ),
        in_specs=[vmem] * 2,
        out_specs=(vmem, vmem),
        compiler_params=pltpu.CompilerParams(vmem_limit_bytes=1024 * 1024),
    )(adjoint, control)
    return from_rows(adjoint, nodes_here), control


def solution(mesh):
    return jax.shard_map(
        body,
        mesh=mesh,
        in_specs=(
            P("nodes", None, ("groups", "cells", "sub")),
            P("nodes", None, ("groups", "cells", "sub")),
            P("nodes", None, None, ("groups", "cells", "sub")),
            P("nodes", None, ("groups", "cells", "sub")),
            P(None, ("cells", "sub")),
            P("nodes"),
            P("nodes", None, ("groups", "cells", "sub")),
            P(None, ("cells", "sub")),
            P(),
            P(),
            P(),
        ),
        out_specs=(P("nodes", None, ("groups", "cells", "sub")), P("groups", None)),
        check_vma=False,
    )
```

time: 25.4 us -> 22.4 us (0.88)
  Pallas kernels: 24 us -> 21.6 us
  local copies, waits for them, and re-layouts: 0.65 us -> 0 us
    pallas_call x1, Pallas kernels: 23.3 us -> 21 us  [body(): pl.pallas_call(functools.partial(kernel, scale), out_shape=(jax.ShapeDtyp...]
    unnamed x2 -> x0, local copies, waits for them, and re-layouts: 0.65 us -> none
where the time goes in v1:
time: 22.4 us; the launch traced here: 22.3 us
  Pallas kernels  21.6 us (96%)
  between operations  0.64 us (3%)
    pallas_call x1, Pallas kernels, body(): pl.pallas_call(functools.partial(kernel, scale), out_shape=(jax.ShapeDtyp...  21 us
    pallas_call x1, Pallas kernels, body(): pl.pallas_call(finish, out_shape=(jax.ShapeDtypeStruct((5, rows, LANES),...  0.62 us

profile of v1, /device:TPU:0, one launch (start us, length us, event | category | flops | bytes accessed | tf_op | source)
XLA Modules:
  0.0 22.3 jit_solution(1936116792982090654)
XLA Ops:
  0.6 21.0 %shard_map.122 = (f32[5,16,128]{2,1,0:T(8,128)S(1)}, f32[3,512]{1,0:T(4,128)S(1)}) custom-call(f32[2]{0:T(128)} %weight_hbm.1, f32[5,16,128]{2,1,0:T(8,128)} %bitcast.49, f32[3,1024]{1,0:T(4,128)} %point_hbm.1, s32[6,1024]{1,0:T(8,128)} %nb_hbm.1, f32[3,4096]{1,0:T(4,128)} %base_hbm.1, bf16[6,25,16,128]{3,2,1,0:T(8,128)(2,1)} %bitcast.44, ...), custom_call_target="tpu_custom_call" | custom-call | tf_op jit(solution)/shard_map/pallas_call | solution.py:507
  21.7 0.6 %shard_map.123 = (f32[5,16,128]{2,1,0:T(8,128)}, f32[3,512]{1,0:T(4,128)}) custom-call(f32[5,16,128]{2,1,0:T(8,128)S(1)} %get-tuple-element.6.adjoint_in, f32[3,512]{1,0:T(4,128)S(1)} %get-tuple-element.7.control_in), custom_call_target="tpu_custom_call" | custom-call | tf_op jit(solution)/shard_map/pallas_call | solution.py:570

commit v2 on v1

--- a/solution.py
+++ b/solution.py
@@ -56,6 +56,7 @@
     wide,
     rel_ref,
     lane_ref,
+    found_ref,
     points,
     cell_rows,
     cell_feat,
@@ -101,6 +102,27 @@
     below, above = cell_at - 1, cell_at + 1
     beside_count = lower.astype(jnp.int32) + upper.astype(jnp.int32)
 
+    adj_load = pltpu.make_async_copy(
+        adj_hbm, wide.at[0, :, pl.ds(rows, rows), :], load_sem.at[0]
+    )
+    adj_load.start()
+    barrier = pltpu.get_barrier_semaphore()
+
+    def greet(device):
+        pl.semaphore_signal(barrier, inc=1, device_id=device, device_id_type=MESH)
+
+    greeted = crew - 1
+    for step in range(1, crew):
+        greet(member((team + step) % crew))
+    greetings = [(lower, {"cells": below}), (upper, {"cells": above})]
+    if subs > 1:
+        first, last = sub_at == 0, sub_at == subs - 1
+        greetings.append((jnp.logical_and(lower, first), {"cells": below, "sub": subs - 1}))
+        greetings.append((jnp.logical_and(upper, last), {"cells": above, "sub": 0}))
+    for exists, device in greetings:
+        pl.when(exists)(functools.partial(greet, device))
+        greeted = greeted + exists.astype(jnp.int32)
+
     base_start = pl.multiple_of(team * base_own, LANES)
     share = pl.ds(base_start, base_own)
     sources = (
@@ -116,7 +138,7 @@
         (7, ffd_weight_hbm.at[:, share], ffd_weight_ref),
         (8, weight_hbm, weight_ref),
     )
-    for group, source, target in sources:
+    for group, source, target in sources[1:]:
         pltpu.make_async_copy(source, target, load_sem.at[group]).start()
 
     def arrive(size, sem):
@@ -129,23 +151,6 @@
     def load_wait(*groups):
         for group in groups:
             arrive(sizes[group], load_sem.at[group])
-
-    barrier = pltpu.get_barrier_semaphore()
-
-    def greet(device):
-        pl.semaphore_signal(barrier, inc=1, device_id=device, device_id_type=MESH)
-
-    greeted = crew - 1
-    for step in range(1, crew):
-        greet(member((team + step) % crew))
-    greetings = [(lower, {"cells": below}), (upper, {"cells": above})]
-    if subs > 1:
-        first, last = sub_at == 0, sub_at == subs - 1
-        greetings.append((jnp.logical_and(lower, first), {"cells": below, "sub": subs - 1}))
-        greetings.append((jnp.logical_and(upper, last), {"cells": above, "sub": 0}))
-    for exists, device in greetings:
-        pl.when(exists)(functools.partial(greet, device))
-        greeted = greeted + exists.astype(jnp.int32)
 
     def tell(stage):
         for exists, other in ((upper, above), (lower, below)):
@@ -191,15 +196,6 @@
         def _():
             halo(sweep, 1).start()
 
-    def halo_wait(sweep):
-        @pl.when(here > 0)
-        def _():
-            halo(sweep, 0).wait_recv()
-
-        @pl.when(here < places - 1)
-        def _():
-            halo(sweep, 1).wait_recv()
-
     def halo_sent():
         both = wide.at[:, :, pl.ds(rows, rows), :]
 
@@ -255,12 +251,14 @@
     features((base_ref[...] - 0.5) * stretch, False)
     base_feat[...] = cell_feat[:, 0:base_own].astype(jnp.bfloat16)
 
-    def build_kernel(step):
+    def build_features(step):
         xyz = point_ref[...] if step == 0 else points[step]
         features((xyz - 0.5) * stretch, True)
         cell_rows[...] = cell_feat[:, 0:cell_count].T.astype(jnp.bfloat16)
+
+    def build_kernel(step, begin, end):
         width = 2 * LANES
-        for left in range(0, base_own, width):
+        for left in range(begin, end, width):
             other = base_feat[:, left : left + width]
             for top in range(0, cell_count, PIECE):
                 mine = cell_rows[top : top + PIECE, :]
@@ -307,63 +305,110 @@
             l_lo[panel, top : top + 2 * ROWS, :] = found_lo
         return carry
 
-    def relax(sweep):
-        pieces, stride = rows // ROWS, ROWS // nodes_here
-        zero = jnp.zeros((ROWS, LANES), jnp.float32)
-        coupled = [[zero] * 5 for _ in range(pieces)]
+    pieces, stride = rows // ROWS, ROWS // nodes_here
+    zero = jnp.zeros((ROWS, LANES), jnp.float32)
+
+    def arrives_late(piece, chunk, far_low, far_high):
+        first_row = chunk + stride * piece
+        last_row = first_row + stride - 1
+        return (far_low and first_row < blocks) or (far_high and last_row >= 2 * blocks)
+
+    def seek(sweep, face, piece, found, chunks):
+        span = slice(piece * ROWS, (piece + 1) * ROWS)
+        rel, lane = rel_ref[face, span, :], lane_ref[face, span, :]
+        for chunk in chunks:
+            match = rel == chunk
+            at = (chunk + stride * piece) * nodes_here
+            for comp in range(5):
+                window = wide[sweep, comp, at : at + ROWS, :]
+                taken = jnp.take_along_axis(window, lane, axis=1)
+                found[comp] = jnp.where(match, taken, found[comp])
+        return found
+
+    def chunk_lists(piece, far):
+        late = [c for c in range(2 * blocks + 1) if arrives_late(piece, c, *far)]
+        return [c for c in range(2 * blocks + 1) if c not in late], late
+
+    def relax_early(sweep, far):
         for face in range(off_ref.shape[0]):
             for piece in range(pieces):
-                span = slice(piece * ROWS, (piece + 1) * ROWS)
-                rel, lane = rel_ref[face, span, :], lane_ref[face, span, :]
-                found = [zero] * 5
-                for chunk in range(2 * blocks + 1):
-                    match = rel == chunk
-                    at = (chunk + stride * piece) * nodes_here
-                    for comp in range(5):
-                        window = wide[sweep, comp, at : at + ROWS, :]
-                        taken = jnp.take_along_axis(window, lane, axis=1)
-                        found[comp] = jnp.where(match, taken, found[comp])
+                found = seek(sweep, face, piece, [zero] * 5, chunk_lists(piece, far)[0])
+                for comp in range(5):
+                    found_ref[face, piece, comp] = found[comp]
+
+    def relax_late(sweep, far):
+        for piece in range(pieces):
+            span = slice(piece * ROWS, (piece + 1) * ROWS)
+            coupled = [zero] * 5
+            for face in range(off_ref.shape[0]):
+                found = [found_ref[face, piece, comp] for comp in range(5)]
+                found = seek(sweep, face, piece, found, chunk_lists(piece, far)[1])
                 for a in range(5):
                     for b in range(5):
                         block = off_ref[face, 5 * a + b, span].astype(jnp.float32)
-                        coupled[piece][a] = coupled[piece][a] + block * found[b]
-        result = []
-        for piece in range(pieces):
-            span = slice(piece * ROWS, (piece + 1) * ROWS)
-            rest = [rhs_ref[b, span] - coupled[piece][b] for b in range(5)]
-            totals = []
+                        coupled[a] = coupled[a] + block * found[b]
+            rest = [rhs_ref[b, span] - coupled[b] for b in range(5)]
             for a in range(5):
                 total = inv_ref[5 * a, span] * rest[0]
                 for b in range(1, 5):
                     total = total + inv_ref[5 * a + b, span] * rest[b]
-                totals.append(total)
-            result.append(totals)
-        return result
-
-    build_kernel(0)
+                if sweep + 1 < SWEEPS:
+                    at = rows + piece * ROWS
+                    wide[sweep + 1, a, at : at + ROWS, :] = total
+                else:
+                    out_ref[a, span] = total
+
+    def by_side(work, sweep):
+        for far in sorted({(s == 0, s == subs - 1) for s in range(subs)}):
+            same = jnp.logical_and(
+                (sub_at == 0) == far[0], (sub_at == subs - 1) == far[1]
+            )
+            pl.when(same)(functools.partial(work, sweep, far))
+
+    def halo_near(sweep):
+        @pl.when(sub_at > 0)
+        def _():
+            halo(sweep, 0).wait_recv()
+
+        @pl.when(sub_at < subs - 1)
+        def _():
+            halo(sweep, 1).wait_recv()
+
+    def halo_far(sweep):
+        @pl.when(jnp.logical_and(sub_at == 0, here > 0))
+        def _():
+            halo(sweep, 0).wait_recv()
+
+        @pl.when(jnp.logical_and(sub_at == subs - 1, here < places - 1))
+        def _():
+            halo(sweep, 1).wait_recv()
+
+    split = max(base_own // 2 // (2 * LANES), 1) * 2 * LANES
+    halo_near(0)
+    by_side(relax_early, 0)
+    build_features(0)
+    build_kernel(0, 0, base_own)
     load_wait(4, 5)
-    halo_wait(0)
-    result = relax(0)
-    for piece, totals in enumerate(result):
-        for a in range(5):
-            wide[1, a, rows + piece * ROWS : rows + (piece + 1) * ROWS, :] = totals[a]
+    halo_far(0)
+    by_side(relax_late, 0)
     halo_start(1)
     if cells > 2:
         hear(0)
         tell(1)
     for step in range(1, subs):
         point_copy(step).wait_recv()
-        build_kernel(step)
+        build_features(step)
+        build_kernel(step, 0, split if step == subs - 1 else base_own)
     load_wait(6, 7, 8)
-    halo_wait(1)
-    result = relax(1)
-    for piece, totals in enumerate(result):
-        span = slice(piece * ROWS, (piece + 1) * ROWS)
-        for k in range(3):
-            total = totals[0] * sens_ref[k, span].astype(jnp.float32)
-            for a in range(1, 5):
-                total = total + totals[a] * sens_ref[3 * a + k, span].astype(jnp.float32)
-            sens_rows[k, span, :] = total
+    halo_near(1)
+    by_side(relax_early, 1)
+    halo_far(1)
+    by_side(relax_late, 1)
+    for k in range(3):
+        total = out_ref[0] * sens_ref[k].astype(jnp.float32)
+        for a in range(1, 5):
+            total = total + out_ref[a] * sens_ref[3 * a + k].astype(jnp.float32)
+        sens_rows[k] = total
     for k in range(3):
         total = weight_ref[0] * sens_rows[k, pl.ds(0, blocks, stride=nodes_here), :]
         for n in range(1, nodes_here):
@@ -382,13 +427,12 @@
 
     for step in range(1, crew):
         sens_copy(step).start()
-    for piece, totals in enumerate(result):
-        for a in range(5):
-            out_ref[a, piece * ROWS : (piece + 1) * ROWS, :] = totals[a]
     for stage in range(2, cells - 1):
         hear(stage - 1)
         tell(stage)
     sens_mat[...] = jnp.zeros_like(sens_mat)
+    if subs > 1:
+        build_kernel(subs - 1, split, base_own)
     lax.fori_loop(0, panels, build_lattice, 0)
     arrive(sens_slots.at[pl.ds(0, crew - 1)], sens_recv)
     for step in range(subs):
@@ -526,6 +570,7 @@
             pltpu.VMEM((SWEEPS, 5, 3 * rows, LANES), f32),
             pltpu.VMEM((faces, rows, LANES), jnp.int32),
             pltpu.VMEM((faces, rows, LANES), jnp.int32),
+            pltpu.VMEM((faces, rows // ROWS, 5, ROWS, LANES), f32),
             pltpu.VMEM((subs, 3, cell_count), f32),
             pltpu.VMEM((cell_count, 24), bf16),
             pltpu.VMEM((24, max(cell_count, base_own)), f32),

time: 22.4 us -> 22 us (0.982)
  Pallas kernels: 21.6 us -> 21.2 us
    pallas_call x1, Pallas kernels: 21 us -> 20.6 us  [body(): pl.pallas_call(functools.partial(kernel, scale), out_shape=(jax.ShapeDtyp...]
where the time goes in v2:
time: 22 us; the launch traced here: 21.8 us
  Pallas kernels  21.2 us (96%)
  between operations  0.64 us (3%)
    pallas_call x1, Pallas kernels, body(): pl.pallas_call(functools.partial(kernel, scale), out_shape=(jax.ShapeDtyp...  20.6 us
    pallas_call x1, Pallas kernels, body(): pl.pallas_call(finish, out_shape=(jax.ShapeDtypeStruct((5, rows, LANES),...  0.62 us

profile of v2, /device:TPU:0, one launch (start us, length us, event | category | flops | bytes accessed | tf_op | source)
XLA Modules:
  0.0 21.8 jit_solution(13649188517603153835)
XLA Ops:
  0.6 20.6 %shard_map.122 = (f32[5,16,128]{2,1,0:T(8,128)S(1)}, f32[3,512]{1,0:T(4,128)S(1)}) custom-call(f32[2]{0:T(128)} %weight_hbm.1, f32[5,16,128]{2,1,0:T(8,128)} %bitcast.49, f32[3,1024]{1,0:T(4,128)} %point_hbm.1, s32[6,1024]{1,0:T(8,128)} %nb_hbm.1, f32[3,4096]{1,0:T(4,128)} %base_hbm.1, bf16[6,25,16,128]{3,2,1,0:T(8,128)(2,1)} %bitcast.44, ...), custom_call_target="tpu_custom_call" | custom-call | tf_op jit(solution)/shard_map/pallas_call | solution.py:551
  21.2 0.6 %shard_map.123 = (f32[5,16,128]{2,1,0:T(8,128)}, f32[3,512]{1,0:T(4,128)}) custom-call(f32[5,16,128]{2,1,0:T(8,128)S(1)} %get-tuple-element.6.adjoint_in, f32[3,512]{1,0:T(4,128)S(1)} %get-tuple-element.7.control_in), custom_call_target="tpu_custom_call" | custom-call | tf_op jit(solution)/shard_map/pallas_call | solution.py:615

commit v3 on v2

--- a/solution.py
+++ b/solution.py
@@ -95,9 +95,6 @@
     def member(index):
         return {"nodes": index // subs, "sub": index % subs}
 
-    def anyone(index):
-        return dict(member(index % crew), cells=index // crew)
-
     lower, upper = cell_at > 0, cell_at < cells - 1
     below, above = cell_at - 1, cell_at + 1
     beside_count = lower.astype(jnp.int32) + upper.astype(jnp.int32)
@@ -211,8 +208,8 @@
         return pltpu.make_async_remote_copy(
             src_ref=point_ref,
             dst_ref=points.at[step],
-            send_sem=point_send.at[step],
-            recv_sem=point_recv.at[step],
+            send_sem=point_send.at[step - 1],
+            recv_sem=point_recv.at[step - 1],
             device_id={"sub": (sub_at + step) % subs},
             device_id_type=MESH,
         )
@@ -256,8 +253,9 @@
         features((xyz - 0.5) * stretch, True)
         cell_rows[...] = cell_feat[:, 0:cell_count].T.astype(jnp.bfloat16)
 
+    width = 2 * LANES
+
     def build_kernel(step, begin, end):
-        width = 2 * LANES
         for left in range(begin, end, width):
             other = base_feat[:, left : left + width]
             for top in range(0, cell_count, PIECE):
@@ -383,11 +381,20 @@
         def _():
             halo(sweep, 1).wait_recv()
 
-    split = max(base_own // 2 // (2 * LANES), 1) * 2 * LANES
+    panel_pairs = base_own // width
+    first_cut, second_cut = ((panel_pairs * part // 4) * width for part in (1, 2))
+
+    def early_with(step, begin, end):
+        def work(sweep, far):
+            build_kernel(step, begin, end)
+            relax_early(sweep, far)
+
+        return work
+
+    build_features(0)
+    build_kernel(0, 0, second_cut)
     halo_near(0)
-    by_side(relax_early, 0)
-    build_features(0)
-    build_kernel(0, 0, base_own)
+    by_side(early_with(0, second_cut, base_own), 0)
     load_wait(4, 5)
     halo_far(0)
     by_side(relax_late, 0)
@@ -398,10 +405,10 @@
     for step in range(1, subs):
         point_copy(step).wait_recv()
         build_features(step)
-        build_kernel(step, 0, split if step == subs - 1 else base_own)
+        build_kernel(step, 0, first_cut if step == subs - 1 else base_own)
     load_wait(6, 7, 8)
     halo_near(1)
-    by_side(relax_early, 1)
+    by_side(early_with(subs - 1, first_cut, second_cut if subs > 1 else first_cut), 1)
     halo_far(1)
     by_side(relax_late, 1)
     for k in range(3):
@@ -415,24 +422,29 @@
             total = total + weight_ref[n] * sens_rows[k, pl.ds(n, blocks, stride=nodes_here), :]
         sens_slots[team, k] = total
 
-    def sens_copy(step):
+    def sens_copy(node_step, sub_step):
         return pltpu.make_async_remote_copy(
             src_ref=sens_slots.at[team],
             dst_ref=sens_slots.at[team],
             send_sem=sens_send,
             recv_sem=sens_recv,
-            device_id=member((team + step) % crew),
+            device_id={
+                "nodes": (node_at + node_step) % nodes,
+                "sub": (sub_at + sub_step) % subs,
+            },
             device_id_type=MESH,
         )
 
-    for step in range(1, crew):
-        sens_copy(step).start()
+    crew_steps = [(n, s) for n in range(1, nodes) for s in range(subs)]
+    crew_steps += [(0, s) for s in range(1, subs)]
+    for node_step, sub_step in crew_steps:
+        sens_copy(node_step, sub_step).start()
     for stage in range(2, cells - 1):
         hear(stage - 1)
         tell(stage)
     sens_mat[...] = jnp.zeros_like(sens_mat)
     if subs > 1:
-        build_kernel(subs - 1, split, base_own)
+        build_kernel(subs - 1, second_cut, base_own)
     lax.fori_loop(0, panels, build_lattice, 0)
     arrive(sens_slots.at[pl.ds(0, crew - 1)], sens_recv)
     for step in range(subs):
@@ -471,20 +483,26 @@
             0:3, block * LANES : (block + 1) * LANES
         ]
 
-    def grad_copy(step):
+    def grad_copy(cell_step, node_step, sub_step):
         return pltpu.make_async_remote_copy(
             src_ref=grad_slots.at[me],
             dst_ref=grad_slots.at[me],
             send_sem=grad_send,
             recv_sem=grad_recv,
-            device_id=anyone((me + step) % everyone),
+            device_id={
+                "cells": (cell_at + cell_step) % cells,
+                "nodes": (node_at + node_step) % nodes,
+                "sub": (sub_at + sub_step) % subs,
+            },
             device_id_type=MESH,
         )
 
     if cells > 1:
         hear(cells - 2)
-    for step in range(1, everyone):
-        grad_copy(step).start()
+    all_steps = [(c,) + step for c in range(1, cells) for step in [(0, 0)] + crew_steps]
+    all_steps += [(0,) + step for step in crew_steps]
+    for steps in all_steps:
+        grad_copy(*steps).start()
     halo_sent()
     for step in range(1, subs):
         point_copy(step).wait_send()
@@ -586,8 +604,8 @@
             dma((9,)),
             dma((2,)),
             dma((SWEEPS, 2)),
-            dma((subs,)),
-            dma((subs,)),
+            dma((max(subs - 1, 1),)),
+            dma((max(subs - 1, 1),)),
             dma,
             dma,
             dma,

time: 22 us -> 21.1 us (0.959)
  Pallas kernels: 21.2 us -> 20.3 us
    pallas_call x1, Pallas kernels: 20.6 us -> 19.7 us  [body(): pl.pallas_call(functools.partial(kernel, scale), out_shape=(jax.ShapeDtyp...]
where the time goes in v3:
time: 21.1 us; the launch traced here: 21 us
  Pallas kernels  20.3 us (96%)
  between operations  0.64 us (3%)
    pallas_call x1, Pallas kernels, body(): pl.pallas_call(functools.partial(kernel, scale), out_shape=(jax.ShapeDtyp...  19.7 us
    pallas_call x1, Pallas kernels, body(): pl.pallas_call(finish, out_shape=(jax.ShapeDtypeStruct((5, rows, LANES),...  0.62 us

profile of v3, /device:TPU:0, one launch (start us, length us, event | category | flops | bytes accessed | tf_op | source)
XLA Modules:
  0.0 21.0 jit_solution(2328697741437637911)
XLA Ops:
  0.6 19.7 %shard_map.122 = (f32[5,16,128]{2,1,0:T(8,128)S(1)}, f32[3,512]{1,0:T(4,128)S(1)}) custom-call(f32[2]{0:T(128)} %weight_hbm.1, f32[5,16,128]{2,1,0:T(8,128)} %bitcast.49, f32[3,1024]{1,0:T(4,128)} %point_hbm.1, s32[6,1024]{1,0:T(8,128)} %nb_hbm.1, f32[3,4096]{1,0:T(4,128)} %base_hbm.1, bf16[6,25,16,128]{3,2,1,0:T(8,128)(2,1)} %bitcast.44, ...), custom_call_target="tpu_custom_call" | custom-call | tf_op jit(solution)/shard_map/pallas_call | solution.py:569
  20.3 0.6 %shard_map.123 = (f32[5,16,128]{2,1,0:T(8,128)}, f32[3,512]{1,0:T(4,128)}) custom-call(f32[5,16,128]{2,1,0:T(8,128)S(1)} %get-tuple-element.6.adjoint_in, f32[3,512]{1,0:T(4,128)S(1)} %get-tuple-element.7.control_in), custom_call_target="tpu_custom_call" | custom-call | tf_op jit(solution)/shard_map/pallas_call | solution.py:633

commit v4 on v3

--- a/solution.py
+++ b/solution.py
@@ -79,6 +79,7 @@
     grad_send,
     grad_recv,
     known,
+    met,
 ):
     cells, subs, nodes = (lax.axis_size(a) for a in ("cells", "sub", "nodes"))
     cell_at, sub_at, node_at = (lax.axis_index(a) for a in ("cells", "sub", "nodes"))
@@ -92,9 +93,6 @@
     base_own = base_ref.shape[1]
     panels = base_own // LANES
 
-    def member(index):
-        return {"nodes": index // subs, "sub": index % subs}
-
     lower, upper = cell_at > 0, cell_at < cells - 1
     below, above = cell_at - 1, cell_at + 1
     beside_count = lower.astype(jnp.int32) + upper.astype(jnp.int32)
@@ -108,9 +106,12 @@
     def greet(device):
         pl.semaphore_signal(barrier, inc=1, device_id=device, device_id_type=MESH)
 
-    greeted = crew - 1
-    for step in range(1, crew):
-        greet(member((team + step) % crew))
+    contact = sub_at == subs - 1
+    greeted = subs - 1 + contact.astype(jnp.int32) * (nodes - 1)
+    for step in range(1, nodes):
+        pl.when(contact)(functools.partial(greet, {"nodes": (node_at + step) % nodes}))
+    for step in range(1, subs):
+        greet({"sub": (sub_at + step) % subs})
     greetings = [(lower, {"cells": below}), (upper, {"cells": above})]
     if subs > 1:
         first, last = sub_at == 0, sub_at == subs - 1
@@ -164,6 +165,35 @@
     def hear(stage):
         pl.semaphore_wait(known.at[stage], beside_count)
 
+    def announce():
+        @pl.when(contact)
+        def _():
+            for step in range(1, nodes):
+                pl.semaphore_signal(
+                    met.at[0],
+                    inc=1,
+                    device_id={"nodes": (node_at + step) % nodes},
+                    device_id_type=MESH,
+                )
+
+    def pass_on():
+        @pl.when(contact)
+        def _():
+            if nodes > 1:
+                pl.semaphore_wait(met.at[0], nodes - 1)
+            for step in range(1, subs):
+                pl.semaphore_signal(
+                    met.at[1],
+                    inc=1,
+                    device_id={"sub": (sub_at + step) % subs},
+                    device_id_type=MESH,
+                )
+
+    def crew_known():
+        @pl.when(jnp.logical_not(contact))
+        def _():
+            pl.semaphore_wait(met.at[1], 1)
+
     @pl.when(here == 0)
     def _():
         wide[:, :, 0:rows, :] = jnp.zeros((SWEEPS, 5, rows, LANES), jnp.float32)
@@ -219,7 +249,7 @@
     halo_start(0)
     for step in range(1, subs):
         point_copy(step).start()
-    tell(0)
+    announce()
 
     load_wait(2, 3)
     first_cell = here * cell_count
@@ -292,15 +322,19 @@
 
         index, hi, lo = spread(index, jnp.int16), spread(hi, jnp.bfloat16), spread(lo, jnp.bfloat16)
         row = lax.broadcasted_iota(jnp.int32, tall, 0).astype(jnp.int16)
-        for top in range(0, FFD, 2 * ROWS):
-            found_hi = found_lo = jnp.zeros(tall, jnp.bfloat16)
-            here_row = row + jnp.int16(top)
-            for s in range(slots):
-                match = index[s] == here_row
-                found_hi = jnp.where(match, hi[s], found_hi)
-                found_lo = jnp.where(match, lo[s], found_lo)
-            l_hi[panel, top : top + 2 * ROWS, :] = found_hi
-            l_lo[panel, top : top + 2 * ROWS, :] = found_lo
+        for column in range(0, FFD, LANES):
+            rows_hi, rows_lo = [], []
+            for top in range(column, column + LANES, 2 * ROWS):
+                found_hi = found_lo = jnp.zeros(tall, jnp.bfloat16)
+                here_row = row + jnp.int16(top)
+                for s in range(slots):
+                    match = index[s] == here_row
+                    found_hi = jnp.where(match, hi[s], found_hi)
+                    found_lo = jnp.where(match, lo[s], found_lo)
+                rows_hi.append(found_hi)
+                rows_lo.append(found_lo)
+            l_hi[column // LANES, at, :] = jnp.concatenate(rows_hi, axis=0).T
+            l_lo[column // LANES, at, :] = jnp.concatenate(rows_lo, axis=0).T
         return carry
 
     pieces, stride = rows // ROWS, ROWS // nodes_here
@@ -382,7 +416,7 @@
             halo(sweep, 1).wait_recv()
 
     panel_pairs = base_own // width
-    first_cut, second_cut = ((panel_pairs * part // 4) * width for part in (1, 2))
+    second_cut, third_cut = ((panel_pairs * part // 4) * width for part in (2, 3))
 
     def early_with(step, begin, end):
         def work(sweep, far):
@@ -394,21 +428,23 @@
     build_features(0)
     build_kernel(0, 0, second_cut)
     halo_near(0)
-    by_side(early_with(0, second_cut, base_own), 0)
+    by_side(early_with(0, second_cut, third_cut), 0)
+    pass_on()
     load_wait(4, 5)
     halo_far(0)
     by_side(relax_late, 0)
     halo_start(1)
-    if cells > 2:
-        hear(0)
-        tell(1)
+    crew_known()
+    tell(0)
+    build_kernel(0, third_cut, base_own)
     for step in range(1, subs):
         point_copy(step).wait_recv()
         build_features(step)
-        build_kernel(step, 0, first_cut if step == subs - 1 else base_own)
+        if step < subs - 1:
+            build_kernel(step, 0, base_own)
     load_wait(6, 7, 8)
     halo_near(1)
-    by_side(early_with(subs - 1, first_cut, second_cut if subs > 1 else first_cut), 1)
+    by_side(early_with(subs - 1, 0, second_cut if subs > 1 else 0), 1)
     halo_far(1)
     by_side(relax_late, 1)
     for k in range(3):
@@ -439,12 +475,15 @@
     crew_steps += [(0, s) for s in range(1, subs)]
     for node_step, sub_step in crew_steps:
         sens_copy(node_step, sub_step).start()
+    if cells > 2:
+        hear(0)
+        tell(1)
+    sens_mat[...] = jnp.zeros_like(sens_mat)
+    if subs > 1:
+        build_kernel(subs - 1, second_cut, base_own)
     for stage in range(2, cells - 1):
         hear(stage - 1)
         tell(stage)
-    sens_mat[...] = jnp.zeros_like(sens_mat)
-    if subs > 1:
-        build_kernel(subs - 1, second_cut, base_own)
     lax.fori_loop(0, panels, build_lattice, 0)
     arrive(sens_slots.at[pl.ds(0, crew - 1)], sens_recv)
     for step in range(subs):
@@ -461,48 +500,50 @@
                 sens_mat[ROWS + k : ROWS + k + 1, at : at + LANES] = lo[block : block + 1, :]
 
     left = sens_mat[...].astype(jnp.bfloat16)
-    contract = (((1,), (1,)), ((), ()))
-    own = jnp.zeros((2 * ROWS, FFD), jnp.float32)
-    grads = []
+    pieces_hi, pieces_lo = [], []
     for pair in range(0, panels, 2):
         product = jnp.zeros((2 * ROWS, 2 * LANES), jnp.float32)
         for table in (k_hi, k_lo):
             both = jnp.concatenate([table[pair], table[pair + 1]], axis=1)
             product = product + jnp.dot(left, both, preferred_element_type=jnp.float32)
-        grads.append((product[0:ROWS] + product[ROWS:]) * scale)
-    for pair in range(0, panels, 2):
-        base_grad = grads[pair // 2]
+        base_grad = (product[0:ROWS] + product[ROWS:]) * scale
         hi = base_grad.astype(jnp.bfloat16).astype(jnp.float32)
-        sides = jnp.concatenate([hi, base_grad - hi], axis=0).astype(jnp.bfloat16)
+        pieces_hi.append(hi)
+        pieces_lo.append(base_grad - hi)
+    left = jnp.concatenate(
+        [jnp.concatenate(pieces_hi, axis=1), jnp.concatenate(pieces_lo, axis=1)], axis=0
+    ).astype(jnp.bfloat16)
+    owns = []
+    for pair in range(0, FFD // LANES, 2):
+        product = jnp.zeros((2 * ROWS, 2 * LANES), jnp.float32)
         for table in (l_hi, l_lo):
             both = jnp.concatenate([table[pair], table[pair + 1]], axis=1)
-            own = own + lax.dot_general(sides, both, contract, preferred_element_type=jnp.float32)
-    own = own[0:ROWS] + own[ROWS:]
+            product = product + jnp.dot(left, both, preferred_element_type=jnp.float32)
+        owns.append(product[0:ROWS] + product[ROWS:])
+    own = jnp.concatenate(owns, axis=1)
     for block in range(FFD // LANES):
         grad_slots[me, 3 * block : 3 * block + 3, :] = own[
             0:3, block * LANES : (block + 1) * LANES
         ]
 
-    def grad_copy(cell_step, node_step, sub_step):
+    def grad_copy(slot):
         return pltpu.make_async_remote_copy(
             src_ref=grad_slots.at[me],
             dst_ref=grad_slots.at[me],
             send_sem=grad_send,
             recv_sem=grad_recv,
             device_id={
-                "cells": (cell_at + cell_step) % cells,
-                "nodes": (node_at + node_step) % nodes,
-                "sub": (sub_at + sub_step) % subs,
+                "cells": slot // crew,
+                "nodes": slot % crew // subs,
+                "sub": slot % subs,
             },
             device_id_type=MESH,
         )
 
     if cells > 1:
         hear(cells - 2)
-    all_steps = [(c,) + step for c in range(1, cells) for step in [(0, 0)] + crew_steps]
-    all_steps += [(0,) + step for step in crew_steps]
-    for steps in all_steps:
-        grad_copy(*steps).start()
+    for slot in range(everyone):
+        pl.when(slot != me)(grad_copy(slot).start)
     halo_sent()
     for step in range(1, subs):
         point_copy(step).wait_send()
@@ -595,8 +636,8 @@
             pltpu.VMEM((24, base_own), bf16),
             pltpu.VMEM((panels, subs * cell_count, LANES), bf16),
             pltpu.VMEM((panels, subs * cell_count, LANES), bf16),
-            pltpu.VMEM((panels, FFD, LANES), bf16),
-            pltpu.VMEM((panels, FFD, LANES), bf16),
+            pltpu.VMEM((FFD // LANES, base_own, LANES), bf16),
+            pltpu.VMEM((FFD // LANES, base_own, LANES), bf16),
             pltpu.VMEM((3, rows, LANES), f32),
             pltpu.VMEM((crew, 3, blocks, LANES), f32),
             pltpu.VMEM((2 * ROWS, subs * cell_count), f32),
@@ -611,6 +652,7 @@
             dma,
             dma,
             pltpu.SemaphoreType.REGULAR((max(cells - 1, 1),)),
+            pltpu.SemaphoreType.REGULAR((2,)),
         ],
         compiler_params=pltpu.CompilerParams(
             collective_id=0, has_side_effects=True, vmem_limit_bytes=16 * 1024 * 1024

time: 21.1 us -> 20.6 us (0.976)
  Pallas kernels: 20.3 us -> 19.9 us
    pallas_call x1, Pallas kernels: 19.7 us -> 19.2 us  [body(): pl.pallas_call(functools.partial(kernel, scale), out_shape=(jax.ShapeDtyp...]
where the time goes in v4:
time: 20.6 us; the launch traced here: 20.5 us
  Pallas kernels  19.9 us (97%)
  between operations  0.64 us (3%)
    pallas_call x1, Pallas kernels, body(): pl.pallas_call(functools.partial(kernel, scale), out_shape=(jax.ShapeDtyp...  19.2 us
    pallas_call x1, Pallas kernels, body(): pl.pallas_call(finish, out_shape=(jax.ShapeDtypeStruct((5, rows, LANES),...  0.62 us

profile of v4, /device:TPU:0, one launch (start us, length us, event | category | flops | bytes accessed | tf_op | source)
XLA Modules:
  0.0 20.5 jit_solution(15980812610272565301)
XLA Ops:
  0.6 19.2 %shard_map.122 = (f32[5,16,128]{2,1,0:T(8,128)S(1)}, f32[3,512]{1,0:T(4,128)S(1)}) custom-call(f32[2]{0:T(128)} %weight_hbm.1, f32[5,16,128]{2,1,0:T(8,128)} %bitcast.49, f32[3,1024]{1,0:T(4,128)} %point_hbm.1, s32[6,1024]{1,0:T(8,128)} %nb_hbm.1, f32[3,4096]{1,0:T(4,128)} %base_hbm.1, bf16[6,25,16,128]{3,2,1,0:T(8,128)(2,1)} %bitcast.44, ...), custom_call_target="tpu_custom_call" | custom-call | tf_op jit(solution)/shard_map/pallas_call | solution.py:610
  19.9 0.6 %shard_map.123 = (f32[5,16,128]{2,1,0:T(8,128)}, f32[3,512]{1,0:T(4,128)}) custom-call(f32[5,16,128]{2,1,0:T(8,128)S(1)} %get-tuple-element.6.adjoint_in, f32[3,512]{1,0:T(4,128)S(1)} %get-tuple-element.7.control_in), custom_call_target="tpu_custom_call" | custom-call | tf_op jit(solution)/shard_map/pallas_call | solution.py:675

commit v5 on v4

--- a/solution.py
+++ b/solution.py
@@ -106,20 +106,16 @@
     def greet(device):
         pl.semaphore_signal(barrier, inc=1, device_id=device, device_id_type=MESH)
 
-    contact = sub_at == subs - 1
-    greeted = subs - 1 + contact.astype(jnp.int32) * (nodes - 1)
-    for step in range(1, nodes):
-        pl.when(contact)(functools.partial(greet, {"nodes": (node_at + step) % nodes}))
+    first, last = sub_at == 0, sub_at == subs - 1
+    down, up = jnp.logical_and(lower, first), jnp.logical_and(upper, last)
+    abroad = [(last, {"nodes": (node_at + step) % nodes}) for step in range(1, nodes)]
+    abroad += [(down, {"cells": below, "sub": subs - 1}), (up, {"cells": above, "sub": 0})]
+    greeted = jnp.int32(subs - 1)
+    for exists, device in abroad:
+        pl.when(exists)(functools.partial(greet, device))
+        greeted = greeted + exists.astype(jnp.int32)
     for step in range(1, subs):
         greet({"sub": (sub_at + step) % subs})
-    greetings = [(lower, {"cells": below}), (upper, {"cells": above})]
-    if subs > 1:
-        first, last = sub_at == 0, sub_at == subs - 1
-        greetings.append((jnp.logical_and(lower, first), {"cells": below, "sub": subs - 1}))
-        greetings.append((jnp.logical_and(upper, last), {"cells": above, "sub": 0}))
-    for exists, device in greetings:
-        pl.when(exists)(functools.partial(greet, device))
-        greeted = greeted + exists.astype(jnp.int32)
 
     base_start = pl.multiple_of(team * base_own, LANES)
     share = pl.ds(base_start, base_own)
@@ -165,34 +161,29 @@
     def hear(stage):
         pl.semaphore_wait(known.at[stage], beside_count)
 
+    def meet(which, device):
+        pl.semaphore_signal(met.at[which], inc=1, device_id=device, device_id_type=MESH)
+
     def announce():
-        @pl.when(contact)
-        def _():
-            for step in range(1, nodes):
-                pl.semaphore_signal(
-                    met.at[0],
-                    inc=1,
-                    device_id={"nodes": (node_at + step) % nodes},
-                    device_id_type=MESH,
-                )
+        for exists, device in abroad:
+            pl.when(exists)(functools.partial(meet, 0, device))
 
     def pass_on():
-        @pl.when(contact)
-        def _():
-            if nodes > 1:
-                pl.semaphore_wait(met.at[0], nodes - 1)
+        expected = greeted - (subs - 1)
+
+        @pl.when(expected > 0)
+        def _():
+            pl.semaphore_wait(met.at[0], expected)
+
+        @pl.when(jnp.logical_or(first, last))
+        def _():
             for step in range(1, subs):
-                pl.semaphore_signal(
-                    met.at[1],
-                    inc=1,
-                    device_id={"sub": (sub_at + step) % subs},
-                    device_id_type=MESH,
-                )
+                meet(1, {"sub": (sub_at + step) % subs})
 
     def crew_known():
-        @pl.when(jnp.logical_not(contact))
-        def _():
-            pl.semaphore_wait(met.at[1], 1)
+        if subs > 1:
+            others = (sub_at != 0).astype(jnp.int32) + (sub_at != subs - 1).astype(jnp.int32)
+            pl.semaphore_wait(met.at[1], others)
 
     @pl.when(here == 0)
     def _():
@@ -202,26 +193,24 @@
     def _():
         wide[:, :, 2 * rows : 3 * rows, :] = jnp.zeros((SWEEPS, 5, rows, LANES), jnp.float32)
 
-    def halo(sweep, side):
+    def halo(sweep, side, top=0, tall=rows):
         other = here + 1 if side == 0 else here - 1
         start = 0 if side == 0 else 2 * rows
         return pltpu.make_async_remote_copy(
-            src_ref=wide.at[sweep, :, pl.ds(rows, rows), :],
-            dst_ref=wide.at[sweep, :, pl.ds(start, rows), :],
+            src_ref=wide.at[sweep, :, pl.ds(rows + top, tall), :],
+            dst_ref=wide.at[sweep, :, pl.ds(start + top, tall), :],
             send_sem=halo_send.at[side],
             recv_sem=halo_recv.at[sweep, side],
             device_id={"cells": other // subs, "sub": other % subs},
             device_id_type=MESH,
         )
 
-    def halo_start(sweep):
-        @pl.when(here < places - 1)
-        def _():
-            halo(sweep, 0).start()
-
-        @pl.when(here > 0)
-        def _():
-            halo(sweep, 1).start()
+    def halo_start(sweep, top, tall):
+        for side, exists in enumerate((here < places - 1, here > 0)):
+
+            @pl.when(exists)
+            def _():
+                halo(sweep, side, top, tall).start()
 
     def halo_sent():
         both = wide.at[:, :, pl.ds(rows, rows), :]
@@ -246,7 +235,7 @@
 
     load_wait(0, 1)
     pl.semaphore_wait(barrier, greeted)
-    halo_start(0)
+    halo_start(0, 0, rows)
     for step in range(1, subs):
         point_copy(step).start()
     announce()
@@ -281,7 +270,7 @@
     def build_features(step):
         xyz = point_ref[...] if step == 0 else points[step]
         features((xyz - 0.5) * stretch, True)
-        cell_rows[...] = cell_feat[:, 0:cell_count].T.astype(jnp.bfloat16)
+        cell_rows[step] = cell_feat[:, 0:cell_count].T.astype(jnp.bfloat16)
 
     width = 2 * LANES
 
@@ -289,7 +278,7 @@
         for left in range(begin, end, width):
             other = base_feat[:, left : left + width]
             for top in range(0, cell_count, PIECE):
-                mine = cell_rows[top : top + PIECE, :]
+                mine = cell_rows[step, top : top + PIECE, :]
                 target = slice(step * cell_count + top, step * cell_count + top + PIECE)
                 squared = jnp.dot(mine, other, preferred_element_type=jnp.float32)
                 squared = jnp.maximum(squared, 1e-20)
@@ -302,8 +291,8 @@
                     k_hi[left // LANES + side, target, :] = hi
                     k_lo[left // LANES + side, target, :] = lo
 
-    def build_lattice(panel, carry):
-        at = pl.ds(pl.multiple_of(panel * LANES, LANES), LANES)
+    def build_lattice(panel):
+        at = slice(panel * LANES, (panel + 1) * LANES)
         index, weight = ffd_index_ref[:, at], ffd_weight_ref[:, at]
         slots = index.shape[0]
         slot = lax.broadcasted_iota(jnp.int32, index.shape, 0)
@@ -335,7 +324,6 @@
                 rows_lo.append(found_lo)
             l_hi[column // LANES, at, :] = jnp.concatenate(rows_hi, axis=0).T
             l_lo[column // LANES, at, :] = jnp.concatenate(rows_lo, axis=0).T
-        return carry
 
     pieces, stride = rows // ROWS, ROWS // nodes_here
     zero = jnp.zeros((ROWS, LANES), jnp.float32)
@@ -389,6 +377,8 @@
                     wide[sweep + 1, a, at : at + ROWS, :] = total
                 else:
                     out_ref[a, span] = total
+            if sweep + 1 < SWEEPS:
+                halo_start(sweep + 1, piece * ROWS, ROWS)
 
     def by_side(work, sweep):
         for far in sorted({(s == 0, s == subs - 1) for s in range(subs)}):
@@ -433,15 +423,14 @@
     load_wait(4, 5)
     halo_far(0)
     by_side(relax_late, 0)
-    halo_start(1)
     crew_known()
     tell(0)
-    build_kernel(0, third_cut, base_own)
     for step in range(1, subs):
         point_copy(step).wait_recv()
         build_features(step)
-        if step < subs - 1:
-            build_kernel(step, 0, base_own)
+    build_kernel(0, third_cut, base_own)
+    for step in range(1, subs - 1):
+        build_kernel(step, 0, base_own)
     load_wait(6, 7, 8)
     halo_near(1)
     by_side(early_with(subs - 1, 0, second_cut if subs > 1 else 0), 1)
@@ -481,10 +470,11 @@
     sens_mat[...] = jnp.zeros_like(sens_mat)
     if subs > 1:
         build_kernel(subs - 1, second_cut, base_own)
+    for panel in range(panels):
+        build_lattice(panel)
     for stage in range(2, cells - 1):
         hear(stage - 1)
         tell(stage)
-    lax.fori_loop(0, panels, build_lattice, 0)
     arrive(sens_slots.at[pl.ds(0, crew - 1)], sens_recv)
     for step in range(subs):
         whose = (sub_at - step + subs) % subs
@@ -631,7 +621,7 @@
             pltpu.VMEM((faces, rows, LANES), jnp.int32),
             pltpu.VMEM((faces, rows // ROWS, 5, ROWS, LANES), f32),
             pltpu.VMEM((subs, 3, cell_count), f32),
-            pltpu.VMEM((cell_count, 24), bf16),
+            pltpu.VMEM((subs, cell_count, 24), bf16),
             pltpu.VMEM((24, max(cell_count, base_own)), f32),
             pltpu.VMEM((24, base_own), bf16),
             pltpu.VMEM((panels, subs * cell_count, LANES), bf16),

time: 20.6 us -> 20.1 us (0.976)
  Pallas kernels: 19.9 us -> 19.4 us
    pallas_call x1, Pallas kernels: 19.2 us -> 18.7 us  [body(): pl.pallas_call(functools.partial(kernel, scale), out_shape=(jax.ShapeDtyp...]
where the time goes in v5:
time: 20.1 us; the launch traced here: 20 us
  Pallas kernels  19.4 us (97%)
  between operations  0.64 us (3%)
    pallas_call x1, Pallas kernels, body(): pl.pallas_call(functools.partial(kernel, scale), out_shape=(jax.ShapeDtyp...  18.7 us
    pallas_call x1, Pallas kernels, body(): pl.pallas_call(finish, out_shape=(jax.ShapeDtypeStruct((5, rows, LANES),...  0.62 us

profile of v5, /device:TPU:0, one launch (start us, length us, event | category | flops | bytes accessed | tf_op | source)
XLA Modules:
  0.0 20.0 jit_solution(11667494345589433368)
XLA Ops:
  0.6 18.7 %shard_map.122 = (f32[5,16,128]{2,1,0:T(8,128)S(1)}, f32[3,512]{1,0:T(4,128)S(1)}) custom-call(f32[2]{0:T(128)} %weight_hbm.1, f32[5,16,128]{2,1,0:T(8,128)} %bitcast.49, f32[3,1024]{1,0:T(4,128)} %point_hbm.1, s32[6,1024]{1,0:T(8,128)} %nb_hbm.1, f32[3,4096]{1,0:T(4,128)} %base_hbm.1, bf16[6,25,16,128]{3,2,1,0:T(8,128)(2,1)} %bitcast.44, ...), custom_call_target="tpu_custom_call" | custom-call | tf_op jit(solution)/shard_map/pallas_call | solution.py:600
  19.4 0.6 %shard_map.123 = (f32[5,16,128]{2,1,0:T(8,128)}, f32[3,512]{1,0:T(4,128)}) custom-call(f32[5,16,128]{2,1,0:T(8,128)S(1)} %get-tuple-element.6.adjoint_in, f32[3,512]{1,0:T(4,128)S(1)} %get-tuple-element.7.control_in), custom_call_target="tpu_custom_call" | custom-call | tf_op jit(solution)/shard_map/pallas_call | solution.py:665

commit v6 on v5

--- a/solution.py
+++ b/solution.py
@@ -193,24 +193,32 @@
     def _():
         wide[:, :, 2 * rows : 3 * rows, :] = jnp.zeros((SWEEPS, 5, rows, LANES), jnp.float32)
 
+    pieces, stride = rows // ROWS, ROWS // nodes_here
+
     def halo(sweep, side, top=0, tall=rows):
+        mark = side * pieces + top // ROWS if sweep == 0 else 2 * pieces + side
         other = here + 1 if side == 0 else here - 1
         start = 0 if side == 0 else 2 * rows
         return pltpu.make_async_remote_copy(
             src_ref=wide.at[sweep, :, pl.ds(rows + top, tall), :],
             dst_ref=wide.at[sweep, :, pl.ds(start + top, tall), :],
             send_sem=halo_send.at[side],
-            recv_sem=halo_recv.at[sweep, side],
+            recv_sem=halo_recv.at[mark],
             device_id={"cells": other // subs, "sub": other % subs},
             device_id_type=MESH,
         )
 
-    def halo_start(sweep, top, tall):
-        for side, exists in enumerate((here < places - 1, here > 0)):
-
-            @pl.when(exists)
-            def _():
-                halo(sweep, side, top, tall).start()
+    def halo_start(sweep, piece, side):
+        @pl.when(here < places - 1 if side == 0 else here > 0)
+        def _():
+            halo(sweep, side, piece * ROWS, ROWS).start()
+
+    def halo_arrive(sweep, side):
+        if sweep == 0:
+            for piece in range(pieces):
+                halo(sweep, side, piece * ROWS, ROWS).wait_recv()
+        else:
+            halo(sweep, side).wait_recv()
 
     def halo_sent():
         both = wide.at[:, :, pl.ds(rows, rows), :]
@@ -235,7 +243,9 @@
 
     load_wait(0, 1)
     pl.semaphore_wait(barrier, greeted)
-    halo_start(0, 0, rows)
+    for piece in range(pieces):
+        halo_start(0, pieces - 1 - piece, 0)
+        halo_start(0, piece, 1)
     for step in range(1, subs):
         point_copy(step).start()
     announce()
@@ -325,7 +335,6 @@
             l_hi[column // LANES, at, :] = jnp.concatenate(rows_hi, axis=0).T
             l_lo[column // LANES, at, :] = jnp.concatenate(rows_lo, axis=0).T
 
-    pieces, stride = rows // ROWS, ROWS // nodes_here
     zero = jnp.zeros((ROWS, LANES), jnp.float32)
 
     def arrives_late(piece, chunk, far_low, far_high):
@@ -357,7 +366,11 @@
                     found_ref[face, piece, comp] = found[comp]
 
     def relax_late(sweep, far):
-        for piece in range(pieces):
+        for piece in range(pieces - 1, -1, -1) if far == (True, False) else range(pieces):
+            if sweep == 0 and subs > 1:
+                for side, exists in enumerate((here > 0, here < places - 1)):
+                    if far[side]:
+                        pl.when(exists)(halo(0, side, piece * ROWS, ROWS).wait_recv)
             span = slice(piece * ROWS, (piece + 1) * ROWS)
             coupled = [zero] * 5
             for face in range(off_ref.shape[0]):
@@ -378,7 +391,8 @@
                 else:
                     out_ref[a, span] = total
             if sweep + 1 < SWEEPS:
-                halo_start(sweep + 1, piece * ROWS, ROWS)
+                for side in range(2):
+                    halo_start(sweep + 1, piece, side)
 
     def by_side(work, sweep):
         for far in sorted({(s == 0, s == subs - 1) for s in range(subs)}):
@@ -390,20 +404,20 @@
     def halo_near(sweep):
         @pl.when(sub_at > 0)
         def _():
-            halo(sweep, 0).wait_recv()
+            halo_arrive(sweep, 0)
 
         @pl.when(sub_at < subs - 1)
         def _():
-            halo(sweep, 1).wait_recv()
+            halo_arrive(sweep, 1)
 
     def halo_far(sweep):
         @pl.when(jnp.logical_and(sub_at == 0, here > 0))
         def _():
-            halo(sweep, 0).wait_recv()
+            halo_arrive(sweep, 0)
 
         @pl.when(jnp.logical_and(sub_at == subs - 1, here < places - 1))
         def _():
-            halo(sweep, 1).wait_recv()
+            halo_arrive(sweep, 1)
 
     panel_pairs = base_own // width
     second_cut, third_cut = ((panel_pairs * part // 4) * width for part in (2, 3))
@@ -421,7 +435,8 @@
     by_side(early_with(0, second_cut, third_cut), 0)
     pass_on()
     load_wait(4, 5)
-    halo_far(0)
+    if subs == 1:
+        halo_far(0)
     by_side(relax_late, 0)
     crew_known()
     tell(0)
@@ -634,7 +649,7 @@
             pltpu.VMEM((everyone, 3 * FFD // LANES, LANES), f32),
             dma((9,)),
             dma((2,)),
-            dma((SWEEPS, 2)),
+            dma((2 * (rows // ROWS) + 2,)),
             dma((max(subs - 1, 1),)),
             dma((max(subs - 1, 1),)),
             dma,

time: 20.1 us -> 20.1 us (level)
  no operation moved by 1% of the time
where the time goes in v6:
time: 20.1 us; the launch traced here: 19.9 us
  Pallas kernels  19.3 us (96%)
  between operations  0.64 us (3%)
    pallas_call x1, Pallas kernels, body(): pl.pallas_call(functools.partial(kernel, scale), out_shape=(jax.ShapeDtyp...  18.7 us
    pallas_call x1, Pallas kernels, body(): pl.pallas_call(finish, out_shape=(jax.ShapeDtypeStruct((5, rows, LANES),...  0.62 us

profile of v6, /device:TPU:0, one launch (start us, length us, event | category | flops | bytes accessed | tf_op | source)
XLA Modules:
  0.0 19.9 jit_solution(7859150724373036800)
XLA Ops:
  0.6 18.7 %shard_map.122 = (f32[5,16,128]{2,1,0:T(8,128)S(1)}, f32[3,512]{1,0:T(4,128)S(1)}) custom-call(f32[2]{0:T(128)} %weight_hbm.1, f32[5,16,128]{2,1,0:T(8,128)} %bitcast.49, f32[3,1024]{1,0:T(4,128)} %point_hbm.1, s32[6,1024]{1,0:T(8,128)} %nb_hbm.1, f32[3,4096]{1,0:T(4,128)} %base_hbm.1, bf16[6,25,16,128]{3,2,1,0:T(8,128)(2,1)} %bitcast.44, ...), custom_call_target="tpu_custom_call" | custom-call | tf_op jit(solution)/shard_map/pallas_call | solution.py:615
  19.3 0.6 %shard_map.123 = (f32[5,16,128]{2,1,0:T(8,128)}, f32[3,512]{1,0:T(4,128)}) custom-call(f32[5,16,128]{2,1,0:T(8,128)S(1)} %get-tuple-element.6.adjoint_in, f32[3,512]{1,0:T(4,128)S(1)} %get-tuple-element.7.control_in), custom_call_target="tpu_custom_call" | custom-call | tf_op jit(solution)/shard_map/pallas_call | solution.py:680
